TPU v7x, 128 devices: a whole 4x4x4 slice. The times are simulated.
128 devices in a mesh: tm: 16 (over x, y), rows: 8 (over z, core).
Axes of the slice: x: 4, y: 4, z: 4, core: 2. Of those that a mesh axis runs over, the one named last changes fastest.
Arguments:
- features: bfloat16 [64, 128, 48, 256], P('tm', 'rows'), may hold values from -16 to 16
- gamma_one: float32 [256], replicated, may hold values from 0.1 to 1.9
- beta_one: float32 [256], replicated, may hold values from -3 to 3
- weight_one: bfloat16 [3, 3, 3, 256, 256], replicated, may hold values from -0.078125 to 0.078125
- bias_one: float32 [256], replicated, may hold values from -3 to 3
- gamma_two: float32 [256], replicated, may hold values from 0.1 to 1.9
- beta_two: float32 [256], replicated, may hold values from -3 to 3
- weight_two: bfloat16 [3, 3, 3, 256, 256], replicated, may hold values from -0.078125 to 0.078125
- bias_two: float32 [256], replicated, may hold values from -3 to 3
Outputs:
- block_out: bfloat16 [64, 128, 48, 256], P('tm', 'rows')
All inputs are finite; a program needn't handle non-finite values.
Results may differ from a plain program's by a relative error of at most 0.006.
Values may be sent and summed in bfloat16 or wider, within the bound.
A program may use at most 128 MiB of HBM per device.

v0:
```python
import jax
import jax.numpy as jnp
from jax import lax
from jax.sharding import PartitionSpec as P

GROUPS = 32


epsilon = 1e-06


def entering(part, axis, combine, identity):
    place = lax.axis_index(axis)
    gathered = jax.tree.map(lambda a: lax.all_gather(a, axis), part)
    state = jax.tree.map(lambda a, e: jnp.zeros_like(a) + jnp.asarray(e, a.dtype), part, identity)

    def one(step, state):
        return combine(
            state, jax.tree.map(lambda a: lax.dynamic_index_in_dim(a, step, 0, False), gathered)
        )

    return lax.fori_loop(0, place, one, state)


def shifted(block, axis, distance):
    devices = range(lax.axis_size(axis))
    route = [(i - distance, i) for i in devices if i - distance in devices]
    return lax.ppermute(block, axis, route)


def padded(x, sides, width):
    for axis, dim in sides:
        size, length = (lax.axis_size(axis), x.shape[dim])
        up = [(i, (i + 1) % size) for i in range(size - 1)]
        down = [(j, i) for i, j in up]
        last = lax.slice_in_dim(x, length - width, length, axis=dim)
        first = lax.slice_in_dim(x, 0, width, axis=dim)
        before = lax.ppermute(last, axis, up)
        after = lax.ppermute(first, axis, down)
        x = jnp.concatenate([before, x, after], axis=dim)
    return x


def add_pairs(earlier, later):
    return (earlier[0] + later[0], earlier[1] + later[1])


def causal_norm(widened, gain, shift):
    frame_count, row_count, col_count, chan_count = widened.shape
    per_group = chan_count // GROUPS
    flat = widened.reshape(frame_count, row_count * col_count, chan_count)
    frame_sum = jnp.sum(flat, axis=1).reshape(frame_count, GROUPS, per_group).sum(-1)
    frame_square = jnp.sum(flat * flat, axis=1).reshape(frame_count, GROUPS, per_group).sum(-1)
    frame_sum, frame_square = lax.psum((frame_sum, frame_square), "rows")
    span_sum = jnp.sum(frame_sum, axis=0)
    span_square = jnp.sum(frame_square, axis=0)
    empty = jnp.zeros((GROUPS,), jnp.float32)
    before_sum, before_square = entering((span_sum, span_square), "tm", add_pairs, (empty, empty))
    running_one = before_sum[None, :] + jnp.cumsum(frame_sum, axis=0)
    running_two = before_square[None, :] + jnp.cumsum(frame_square, axis=0)
    first_frame = lax.axis_index("tm") * frame_count
    frame_index = (first_frame + jnp.arange(frame_count, dtype=jnp.int32) + 1).astype(jnp.float32)
    entries = (frame_index * float(row_count * lax.axis_size("rows") * col_count * per_group))[
        :, None
    ]
    group_mean = running_one / entries
    group_var = running_two / entries - group_mean * group_mean
    inv_std = lax.rsqrt(group_var + epsilon)
    mean_chan = jnp.repeat(group_mean, per_group, axis=1)[:, None, None, :]
    scale_chan = jnp.repeat(inv_std, per_group, axis=1)[:, None, None, :]
    normed = (widened - mean_chan) * scale_chan * gain + shift
    return jax.nn.silu(normed).astype(jnp.bfloat16)


def causal_conv(activated, weight, bias):
    frame_count, row_count, col_count, chan_count = activated.shape
    earlier = shifted(activated[frame_count - 2 :], "tm", 1)
    extended = jnp.concatenate([earlier, activated], axis=0)
    extended = padded(extended, (("rows", 1),), 1)
    extended = jnp.pad(extended, ((0, 0), (0, 0), (1, 1), (0, 0)))
    matrices = weight.reshape(3, 9 * chan_count, chan_count)
    total = jnp.zeros((frame_count * row_count * col_count, chan_count), jnp.float32)
    for tap_row in range(3):
        pieces = [
            extended[
                tap_time : tap_time + frame_count,
                tap_row : tap_row + row_count,
                tap_col : tap_col + col_count,
                :,
            ]
            for tap_time in range(3)
            for tap_col in range(3)
        ]
        slab = jnp.concatenate(pieces, axis=-1).reshape(
            frame_count * row_count * col_count, 9 * chan_count
        )
        total = total + jnp.dot(slab, matrices[tap_row], preferred_element_type=jnp.float32)
    return total.reshape(frame_count, row_count, col_count, chan_count) + bias


def on_device(
    features, gamma_one, beta_one, weight_one, bias_one, gamma_two, beta_two, weight_two, bias_two
):
    widened = features.astype(jnp.float32)
    first = causal_norm(widened, gamma_one, beta_one)
    between = causal_conv(first, weight_one, bias_one).astype(jnp.bfloat16)
    second = causal_norm(between.astype(jnp.float32), gamma_two, beta_two)
    return (causal_conv(second, weight_two, bias_two) + widened).astype(jnp.bfloat16)


def solution(mesh):
    placed = (P("tm", "rows", None, None), P(), P(), P(), P(), P(), P(), P(), P())
    return jax.shard_map(
        on_device,
        mesh=mesh,
        in_specs=placed,
        out_specs=P("tm", "rows", None, None),
        check_vma=False,
    )
```

profile of v0, /device:TPU:3, one launch (start us, length us, event | category | flops | bytes accessed | tf_op | source)
XLA Modules:
  0.0 252.0 jit_solution(7191280571662384638)
XLA Ops:
  2.3 13.7 %all-reduce.9 = (f32[4,32]{1,0:T(4,128)S(1)}, f32[4,32]{1,0:T(4,128)S(1)}) all-reduce(f32[4,32]{1,0:T(4,128)S(1)} %reduce_sum.109, f32[4,32]{1,0:T(4,128)S(1)} %reduce_sum.112), channel_id=1, replica_groups=mesh['tm'=16,'rows'=8] {'rows'}, use_global_device_ids=true, to_apply=%region_2.0 | all-reduce | flops 256 | bytes 2048 | tf_op jit(solution)/shard_map/psum | solution.py:54
  18.4 27.9 %all-reduce.7 = (f32[512]{0:T(512)S(1)}, f32[512]{0:T(512)S(1)}) all-reduce(f32[512]{0:T(512)S(1)} %dynamic-update-slice, f32[512]{0:T(512)S(1)} %dynamic-update-slice.1), channel_id=2, replica_groups=mesh['tm'=16,'rows'=8] {'tm'}, use_global_device_ids=true, to_apply=%add.2 | all-reduce | flops 1024 | bytes 8192
  51.1 12.9 %collective-permute-done = bf16[2,16,48,256]{3,2,1,0:T(8,128)(2,1)S(1)} collective-permute-done((bf16[2,16,48,256]{3,2,1,0:T(8,128)(2,1)S(1)}, bf16[2,16,48,256]{3,2,1,0:T(8,128)(2,1)S(1)}, u32[]{:S(2)}, u32[]{:S(2)}) %collective-permute-start) | collective-permute-done | bytes 786464 | tf_op jit(solution)/shard_map/ppermute | solution.py:28
  65.7 10.8 %collective-permute-start.1 = (bf16[6,1,48,256]{3,2,1,0:T(8,128)(2,1)}, bf16[6,1,48,256]{3,2,1,0:T(8,128)(2,1)S(1)}, u32[]{:S(2)}, u32[]{:S(2)}) collective-permute-start(bf16[6,1,48,256]{3,2,1,0:T(8,128)(2,1)} %get-tuple-element.169), channel_id=1, source_target_pairs={{0,1},{1,2},{2,3},{3,4},{4,5},{5,6},{6,7},{8,9},{9,10},{10,11},{11... | collective-permute-start | bytes 442376 | tf_op jit(solution)/shard_map/ppermute | solution.py:38
  76.5 3.4 %collective-permute-start.2 = (bf16[6,1,48,256]{3,2,1,0:T(8,128)(2,1)}, bf16[6,1,48,256]{3,2,1,0:T(8,128)(2,1)S(1)}, u32[]{:S(2)}, u32[]{:S(2)}) collective-permute-start(bf16[6,1,48,256]{3,2,1,0:T(8,128)(2,1)} %get-tuple-element.170), channel_id=1, source_target_pairs={{1,0},{2,1},{3,2},{4,3},{5,4},{6,5},{7,6},{9,8},{10,9},{11,10},{12... | collective-permute-start | bytes 442376 | tf_op jit(solution)/shard_map/ppermute | solution.py:39
  83.1 2.6 %fusion.20 = bf16[6,18,50,256]{3,2,1,0:T(8,128)(2,1)S(1)} fusion(bf16[6,1,48,256]{3,2,1,0:T(8,128)(2,1)S(1)} %collective-permute-done.2, bf16[6,1,48,256]{3,2,1,0:T(8,128)(2,1)S(1)} %collective-permute-done.1, bf16[4,16,48,256]{3,2,1,0:T(8,128)(2,1)S(1)} %fusion.11, bf16[2,16,48,256]{3,2,1,0:T(8,128)(2,1)} %copy-done.2), kind=kLoop, calls=%fused_computation.41 | loop fusion | flops 20736000 | bytes 5419008 | tf_op jit(solution)/shard_map/concatenate | solution.py:40
  91.6 2.8 %slice_dynamic-update-slice_fusion.30 = (bf16[4,16,48,2304]{3,2,1,0:T(8,128)(2,1)S(1)}, bf16[4,16,48,2304]{3,2,1,0:T(8,128)(2,1)}, bf16[4,16,48,2304]{3,2,1,0:T(8,128)(2,1)}) fusion(bf16[4,16,48,2304]{3,2,1,0:T(8,128)(2,1)S(1)} %get-tuple-element.172, bf16[6,18,50,256]{3,2,1,0:T(8,128)(2,1)S(1)} %fusion.20, bf16[4,16,48,2304]{3,2,1,0:T(8,128)(2,1)} %get-tuple-element.171, ...), kind=kLoop, calls=%fused_computation.88 | loop fusion | bytes 9437184
  99.4 2.7 %slice_dynamic-update-slice_fusion.27 = (bf16[4,16,48,2304]{3,2,1,0:T(8,128)(2,1)S(1)}, bf16[4,16,48,2304]{3,2,1,0:T(8,128)(2,1)}, bf16[4,16,48,2304]{3,2,1,0:T(8,128)(2,1)}) fusion(bf16[4,16,48,2304]{3,2,1,0:T(8,128)(2,1)S(1)} %slice_dynamic-update-slice_fusion.28, bf16[6,18,50,256]{3,2,1,0:T(8,128)(2,1)S(1)} %fusion.20, ...), kind=kLoop, calls=%fused_computation.85 | loop fusion | bytes 9437184
  105.7 2.4 constant_dynamic-update-slice_fusion
  108.2 2.7 %slice_dynamic-update-slice_fusion.24 = (bf16[4,16,48,2304]{3,2,1,0:T(8,128)(2,1)S(1)}, bf16[4,16,48,2304]{3,2,1,0:T(8,128)(2,1)}, bf16[4,16,48,2304]{3,2,1,0:T(8,128)(2,1)}) fusion(bf16[4,16,48,2304]{3,2,1,0:T(8,128)(2,1)S(1)} %slice_dynamic-update-slice_fusion.25, bf16[6,18,50,256]{3,2,1,0:T(8,128)(2,1)S(1)} %fusion.20, ...), kind=kLoop, calls=%fused_computation.82 | loop fusion | bytes 9437184 | tf_op jit(solution)/shard_map/concatenate | solution.py:94
  110.9 7.3 %fusion.31 = f32[3072,256]{1,0:T(8,128)S(1)} fusion(bf16[3072,2304]{1,0:T(8,128)(2,1)} %bitcast.54, bf16[2304,256]{1,0:T(8,128)(2,1)S(1)} %bitcast.47), kind=kOutput, calls=%fused_computation.123 | convolution fusion | flops 3623878656 | bytes 18481152 | tf_op jit(solution)/shard_map/dot_general | solution.py:97
  118.2 7.9 %convolution_add_fusion.3 = f32[3072,256]{1,0:T(8,128)S(1)} fusion(f32[3072,256]{1,0:T(8,128)S(1)} %fusion.31, bf16[3072,2304]{1,0:T(8,128)(2,1)} %bitcast.51, bf16[2304,256]{1,0:T(8,128)(2,1)S(1)} %bitcast.46), kind=kOutput, calls=%fused_computation.16 | convolution fusion | flops 3624665088 | bytes 21626880 | tf_op jit(solution)/shard_map/dot_general | solution.py:97
  126.1 4.3 %convolution_add_fusion.2 = f32[3072,256]{1,0:T(8,128)S(1)} fusion(f32[3072,256]{1,0:T(8,128)S(1)} %convolution_add_fusion.3, bf16[3072,2304]{1,0:T(8,128)(2,1)S(1)} %bitcast.50, bf16[2304,256]{1,0:T(8,128)(2,1)S(1)} %bitcast.44), kind=kOutput, calls=%fused_computation.15 | convolution fusion | flops 3624665088 | bytes 21626880 | tf_op jit(solution)/shard_map/dot_general | solution.py:97
  131.3 10.9 %all-reduce.8 = (f32[4,32]{1,0:T(4,128)S(1)}, f32[4,32]{1,0:T(4,128)S(1)}) all-reduce(f32[4,32]{1,0:T(4,128)S(1)} %reduce_sum.115, f32[4,32]{1,0:T(4,128)S(1)} %reduce_sum.118), channel_id=1, replica_groups=mesh['tm'=16,'rows'=8] {'rows'}, use_global_device_ids=true, to_apply=%region_14.15 | all-reduce | flops 256 | bytes 2048 | tf_op jit(solution)/shard_map/psum | solution.py:54
  142.7 26.8 %all-reduce.6 = (f32[512]{0:T(512)S(1)}, f32[512]{0:T(512)S(1)}) all-reduce(f32[512]{0:T(512)S(1)} %dynamic-update-slice.2, f32[512]{0:T(512)S(1)} %dynamic-update-slice.3), channel_id=4, replica_groups=mesh['tm'=16,'rows'=8] {'tm'}, use_global_device_ids=true, to_apply=%add.4 | all-reduce | flops 1024 | bytes 8192
  173.7 12.9 %collective-permute-done.3 = bf16[2,16,48,256]{3,2,1,0:T(8,128)(2,1)S(1)} collective-permute-done((bf16[2,16,48,256]{3,2,1,0:T(8,128)(2,1)S(1)}, bf16[2,16,48,256]{3,2,1,0:T(8,128)(2,1)S(1)}, u32[]{:S(2)}, u32[]{:S(2)}) %collective-permute-start.3) | collective-permute-done | bytes 786464 | tf_op jit(solution)/shard_map/ppermute | solution.py:28
  186.7 10.8 %collective-permute-start.4 = (bf16[6,1,48,256]{3,2,1,0:T(8,128)(2,1)S(1)}, bf16[6,1,48,256]{3,2,1,0:T(8,128)(2,1)S(1)}, u32[]{:S(2)}, u32[]{:S(2)}) collective-permute-start(bf16[6,1,48,256]{3,2,1,0:T(8,128)(2,1)S(1)} %get-tuple-element.165), channel_id=1, source_target_pairs={{0,1},{1,2},{2,3},{3,4},{4,5},{5,6},{6,7},{8,9},{9,10},{10,11},{11... | collective-permute-start | bytes 442376 | tf_op jit(solution)/shard_map/ppermute | solution.py:38
  200.2 3.8 %collective-permute-done.5 = bf16[6,1,48,256]{3,2,1,0:T(8,128)(2,1)S(1)} collective-permute-done((bf16[6,1,48,256]{3,2,1,0:T(8,128)(2,1)S(1)}, bf16[6,1,48,256]{3,2,1,0:T(8,128)(2,1)S(1)}, u32[]{:S(2)}, u32[]{:S(2)}) %collective-permute-start.5) | collective-permute-done | bytes 147488 | tf_op jit(solution)/shard_map/ppermute | solution.py:39
  211.5 2.8 %slice_dynamic-update-slice_fusion.6 = (bf16[4,16,48,2304]{3,2,1,0:T(8,128)(2,1)}, bf16[4,16,48,2304]{3,2,1,0:T(8,128)(2,1)S(1)}, bf16[4,16,48,2304]{3,2,1,0:T(8,128)(2,1)}) fusion(bf16[4,16,48,2304]{3,2,1,0:T(8,128)(2,1)} %slice_dynamic-update-slice_fusion.7, bf16[6,18,50,256]{3,2,1,0:T(8,128)(2,1)S(1)} %select_maximum_fusion, ...), kind=kLoop, calls=%fused_computation.62 | loop fusion | bytes 9437184
  219.4 2.8 %slice_dynamic-update-slice_fusion.3 = (bf16[4,16,48,2304]{3,2,1,0:T(8,128)(2,1)}, bf16[4,16,48,2304]{3,2,1,0:T(8,128)(2,1)S(1)}, bf16[4,16,48,2304]{3,2,1,0:T(8,128)(2,1)}) fusion(bf16[4,16,48,2304]{3,2,1,0:T(8,128)(2,1)} %slice_dynamic-update-slice_fusion.4, bf16[6,18,50,256]{3,2,1,0:T(8,128)(2,1)S(1)} %select_maximum_fusion, ...), kind=kLoop, calls=%fused_computation.59 | loop fusion | bytes 9437184
  228.2 2.7 %slice_dynamic-update-slice_fusion = (bf16[4,16,48,2304]{3,2,1,0:T(8,128)(2,1)}, bf16[4,16,48,2304]{3,2,1,0:T(8,128)(2,1)S(1)}, bf16[4,16,48,2304]{3,2,1,0:T(8,128)(2,1)}) fusion(bf16[4,16,48,2304]{3,2,1,0:T(8,128)(2,1)} %slice_dynamic-update-slice_fusion.1, bf16[6,18,50,256]{3,2,1,0:T(8,128)(2,1)S(1)} %select_maximum_fusion, ...), kind=kLoop, calls=%fused_computation.56 | loop fusion | bytes 9437184 | tf_op jit(solution)/shard_map/concatenate | solution.py:94
  230.9 7.4 %fusion.32 = f32[3072,256]{1,0:T(8,128)S(1)} fusion(bf16[3072,2304]{1,0:T(8,128)(2,1)} %bitcast.55, bf16[2304,256]{1,0:T(8,128)(2,1)S(1)} %bitcast.49), kind=kOutput, calls=%fused_computation.124 | convolution fusion | flops 3623878656 | bytes 18481152 | tf_op jit(solution)/shard_map/dot_general | solution.py:97
  238.3 4.3 %convolution_add_fusion.1 = f32[3072,256]{1,0:T(8,128)S(1)} fusion(f32[3072,256]{1,0:T(8,128)S(1)} %fusion.32, bf16[3072,2304]{1,0:T(8,128)(2,1)S(1)} %bitcast.52, bf16[2304,256]{1,0:T(8,128)(2,1)S(1)} %bitcast.48), kind=kOutput, calls=%fused_computation.14 | convolution fusion | flops 3624665088 | bytes 21626880 | tf_op jit(solution)/shard_map/dot_general | solution.py:97
  242.6 7.4 %convolution_add_fusion = f32[3072,256]{1,0:T(8,128)S(1)} fusion(f32[3072,256]{1,0:T(8,128)S(1)} %convolution_add_fusion.1, bf16[3072,2304]{1,0:T(8,128)(2,1)} %bitcast.53, bf16[2304,256]{1,0:T(8,128)(2,1)S(1)} %bitcast.45), kind=kOutput, calls=%fused_computation.13 | convolution fusion | flops 3624665088 | bytes 21626880 | tf_op jit(solution)/shard_map/dot_general | solution.py:97
  (126 shorter events, 56.7 us)
Async XLA Ops:
  0.0 47.2 %copy-start = (bf16[4,16,48,256]{3,2,1,0:T(8,128)(2,1)S(1)}, bf16[4,16,48,256]{3,2,1,0:T(8,128)(2,1)}, u32[]{:S(2)}) copy-start(bf16[4,16,48,256]{3,2,1,0:T(8,128)(2,1)} %param.13) | copy-start | bytes 4718596
  47.2 32.7 %copy-start.4 = (bf16[3,3,3,256,256]{4,3,2,1,0:T(8,128)(2,1)S(1)}, bf16[3,3,3,256,256]{4,3,2,1,0:T(8,128)(2,1)}, u32[]{:S(2)}) copy-start(bf16[3,3,3,256,256]{4,3,2,1,0:T(8,128)(2,1)} %param.16) | copy-start | bytes 10616836
  49.2 14.8 %collective-permute-start = (bf16[2,16,48,256]{3,2,1,0:T(8,128)(2,1)S(1)}, bf16[2,16,48,256]{3,2,1,0:T(8,128)(2,1)S(1)}, u32[]{:S(2)}, u32[]{:S(2)}) collective-permute-start(bf16[2,16,48,256]{3,2,1,0:T(8,128)(2,1)S(1)} %slice.300), channel_id=1, source_target_pairs={{0,8},{8,16},{16,24},{24,32},{32,40},{40,48},{48,56},{56,64},{64,7... | collective-permute-start | bytes 2359304 | tf_op jit(solution)/shard_map/ppermute | solution.py:28
  64.0 0.9 copy-start.2
  65.7 16.2 %collective-permute-start.1 = (bf16[6,1,48,256]{3,2,1,0:T(8,128)(2,1)}, bf16[6,1,48,256]{3,2,1,0:T(8,128)(2,1)S(1)}, u32[]{:S(2)}, u32[]{:S(2)}) collective-permute-start(bf16[6,1,48,256]{3,2,1,0:T(8,128)(2,1)} %get-tuple-element.169), channel_id=1, source_target_pairs={{0,1},{1,2},{2,3},{3,4},{4,5},{5,6},{6,7},{8,9},{9,10},{10,11},{11... | collective-permute-start | bytes 442376 | tf_op jit(solution)/shard_map/ppermute | solution.py:38
  76.5 6.7 %collective-permute-start.2 = (bf16[6,1,48,256]{3,2,1,0:T(8,128)(2,1)}, bf16[6,1,48,256]{3,2,1,0:T(8,128)(2,1)S(1)}, u32[]{:S(2)}, u32[]{:S(2)}) collective-permute-start(bf16[6,1,48,256]{3,2,1,0:T(8,128)(2,1)} %get-tuple-element.170), channel_id=1, source_target_pairs={{1,0},{2,1},{3,2},{4,3},{5,4},{6,5},{7,6},{9,8},{10,9},{11,10},{12... | collective-permute-start | bytes 442376 | tf_op jit(solution)/shard_map/ppermute | solution.py:39
  85.8 2.2 copy-start.3
  104.3 1.4 copy-start.10
  104.3 1.4 copy-start.11
  108.2 2.7 %copy-start.8 = (bf16[1,3,3,256,256]{4,3,2,1,0:T(8,128)(2,1)S(1)}, bf16[1,3,3,256,256]{4,3,2,1,0:T(8,128)(2,1)}, u32[]{:S(2)}) copy-start(bf16[1,3,3,256,256]{4,3,2,1,0:T(8,128)(2,1)} %get-tuple-element.125) | copy-start | bytes 3538948
  110.9 7.3 %copy-start.7 = (bf16[1,3,3,256,256]{4,3,2,1,0:T(8,128)(2,1)S(1)}, bf16[1,3,3,256,256]{4,3,2,1,0:T(8,128)(2,1)}, u32[]{:S(2)}) copy-start(bf16[1,3,3,256,256]{4,3,2,1,0:T(8,128)(2,1)} %get-tuple-element.126) | copy-start | bytes 3538948
  118.2 7.9 %copy-start.6 = (bf16[1,3,3,256,256]{4,3,2,1,0:T(8,128)(2,1)S(1)}, bf16[1,3,3,256,256]{4,3,2,1,0:T(8,128)(2,1)}, u32[]{:S(2)}) copy-start(bf16[1,3,3,256,256]{4,3,2,1,0:T(8,128)(2,1)} %get-tuple-element.124) | copy-start | bytes 3538948
  126.1 4.3 %copy-start.9 = (f32[256]{0:T(256)S(1)}, f32[256]{0:T(256)}, u32[]{:S(2)}) copy-start(f32[256]{0:T(256)} %param.17) | copy-start | bytes 3076
  130.4 39.9 %copy-start.12 = (f32[256]{0:T(256)S(1)}, f32[256]{0:T(256)}, u32[]{:S(2)}) copy-start(f32[256]{0:T(256)} %param.19) | copy-start | bytes 3076
  130.4 39.9 %copy-start.13 = (f32[256]{0:T(256)S(1)}, f32[256]{0:T(256)}, u32[]{:S(2)}) copy-start(f32[256]{0:T(256)} %param.18) | copy-start | bytes 3076
  171.5 28.4 %copy-start.5 = (bf16[3,3,3,256,256]{4,3,2,1,0:T(8,128)(2,1)S(1)}, bf16[3,3,3,256,256]{4,3,2,1,0:T(8,128)(2,1)}, u32[]{:S(2)}) copy-start(bf16[3,3,3,256,256]{4,3,2,1,0:T(8,128)(2,1)} %param.20) | copy-start | bytes 10616836
  171.6 15.1 %collective-permute-start.3 = (bf16[2,16,48,256]{3,2,1,0:T(8,128)(2,1)S(1)}, bf16[2,16,48,256]{3,2,1,0:T(8,128)(2,1)S(1)}, u32[]{:S(2)}, u32[]{:S(2)}) collective-permute-start(bf16[2,16,48,256]{3,2,1,0:T(8,128)(2,1)S(1)} %slice.327), channel_id=1, source_target_pairs={{0,8},{8,16},{16,24},{24,32},{32,40},{40,48},{48,56},{56,64},{64,7... | collective-permute-start | bytes 2359304 | tf_op jit(solution)/shard_map/ppermute | solution.py:28
  186.7 13.5 %collective-permute-start.4 = (bf16[6,1,48,256]{3,2,1,0:T(8,128)(2,1)S(1)}, bf16[6,1,48,256]{3,2,1,0:T(8,128)(2,1)S(1)}, u32[]{:S(2)}, u32[]{:S(2)}) collective-permute-start(bf16[6,1,48,256]{3,2,1,0:T(8,128)(2,1)S(1)} %get-tuple-element.165), channel_id=1, source_target_pairs={{0,1},{1,2},{2,3},{3,4},{4,5},{5,6},{6,7},{8,9},{9,10},{10,11},{11... | collective-permute-start | bytes 442376 | tf_op jit(solution)/shard_map/ppermute | solution.py:38
  197.5 6.5 %collective-permute-start.5 = (bf16[6,1,48,256]{3,2,1,0:T(8,128)(2,1)S(1)}, bf16[6,1,48,256]{3,2,1,0:T(8,128)(2,1)S(1)}, u32[]{:S(2)}, u32[]{:S(2)}) collective-permute-start(bf16[6,1,48,256]{3,2,1,0:T(8,128)(2,1)S(1)} %get-tuple-element.166), channel_id=1, source_target_pairs={{1,0},{2,1},{3,2},{4,3},{5,4},{6,5},{7,6},{9,8},{10,9},{11,10},{12... | collective-permute-start | bytes 442376 | tf_op jit(solution)/shard_map/ppermute | solution.py:39
  242.6 7.4 %copy-start.1 = (bf16[4,16,48,256]{3,2,1,0:T(8,128)(2,1)S(1)}, bf16[4,16,48,256]{3,2,1,0:T(8,128)(2,1)}, u32[]{:S(2)}) copy-start(bf16[4,16,48,256]{3,2,1,0:T(8,128)(2,1)} %param.13) | copy-start | bytes 4718596
  242.6 7.4 %copy-start.14 = (f32[256]{0:T(256)S(1)}, f32[256]{0:T(256)}, u32[]{:S(2)}) copy-start(f32[256]{0:T(256)} %param.21) | copy-start | bytes 3076
where the time goes:
time: 257 us; the launch traced here: 252 us
  blocking collectives  79.3 us (31%)
  local copies, waits for them, and re-layouts  48.9 us (19%)
  matrix products  38.5 us (15%)
  starting transfers between devices  31.5 us (12%)
  waiting for transfers between devices  31 us (12%)
  other arithmetic  21.3 us (8%)
    unnamed x2, blocking collectives  54.7 us
    unnamed x60, local copies, waits for them, and re-layouts  39.8 us
    dot_general x6, matrix products, causal_conv(): jnp.dot(slab, matrices[tap_row], preferred_element_type=jnp.float32)  38.5 us
    ppermute x2, waiting for transfers between devices, shifted(): return lax.ppermute(block, axis, route)  25.8 us
    psum x2, blocking collectives, causal_norm(): frame_sum, frame_square = lax.psum((frame_sum, frame_square), 'rows')  24.6 us
    ppermute x2, starting transfers between devices, padded(): before = lax.ppermute(last, axis, up)  21.6 us
    unnamed x6, other arithmetic  6.74 us
    ppermute x2, starting transfers between devices, padded(): after = lax.ppermute(first, axis, down)  5.76 us
  transfers between devices with their start and end apart: 6, of which 4 were waited for; matrix products, arithmetic and copies ran while one was open for 1% of the time, Pallas kernels for 0%

commit v1 on v0

v1 whole, which is shorter than its diff:
```python
import functools

import jax
import jax.numpy as jnp
from jax import lax
from jax.experimental import pallas as pl
from jax.experimental.pallas import tpu as pltpu
from jax.sharding import PartitionSpec as P

MESH = pl.DeviceIdType.MESH
GROUPS = 32
EPSILON = 1e-06
HBM = pl.BlockSpec(memory_space=pltpu.HBM)


def group_sum(x, per_group):
    lane = lax.broadcasted_iota(jnp.int32, x.shape, 1)
    step = 1
    while step < per_group:
        up = pltpu.roll(x, x.shape[1] - step, 1)
        down = pltpu.roll(x, step, 1)
        x = x + jnp.where((lane & step) == 0, up, down)
        step *= 2
    return x


def block_kernel(n_tm, n_rw, frames, rows, cols, chans,
                 feat, g1, b1, w1, c1, g2, b2, w2, c2, out,
                 fx, bx, xn, wa, wb, ob, par, sl, ra, tb, st,
                 lsem, psem, wsem, osem, rsend, rrecv, tsend, trecv, hsend, hrecv):
    tm = lax.axis_index("tm")
    rw = lax.axis_index("rows")
    pix = rows * cols
    per_group = chans // GROUPS

    loads = [pltpu.make_async_copy(feat.at[f], fx.at[2 + f, 1:rows + 1], lsem.at[f]) for f in range(frames)]
    for c in loads:
        c.start()
    small = [pltpu.make_async_copy(p, par.at[i], psem.at[i]) for i, p in enumerate((g1, b1, c1, g2, b2, c2))]
    for c in small:
        c.start()
    taps = [
        pltpu.make_async_copy(w.at[:, e], v.at[:, :, e * chans:(e + 1) * chans], wsem.at[n, e])
        for n, (w, v) in enumerate(((w1, wa), (w2, wb))) for e in range(3)
    ]
    for c in taps:
        c.start()

    tb[...] = jnp.zeros_like(tb)

    barrier = pltpu.get_barrier_semaphore()
    for k in range(1, n_rw):
        pl.semaphore_signal(barrier, 1, device_id=(tm, lax.rem(rw + k, n_rw)), device_id_type=MESH)
    for k in range(1, n_tm):
        pl.semaphore_signal(barrier, 1, device_id=(lax.rem(tm + k, n_tm), rw), device_id_type=MESH)
    for dt in (-1, 1):
        for dr in (-1, 1):
            @pl.when((tm + dt >= 0) & (tm + dt < n_tm) & (rw + dr >= 0) & (rw + dr < n_rw))
            def _():
                pl.semaphore_signal(barrier, 1, device_id=(tm + dt, rw + dr), device_id_type=MESH)

    def frame_sums(z):
        part1 = jnp.sum(z.reshape(z.shape[0] // 8, 8, chans), axis=0)
        part2 = jnp.sum((z * z).reshape(z.shape[0] // 8, 8, chans), axis=0)
        return part1, part2

    def put_sums(which, f, part1, part2):
        sl[which, pl.ds(f, 1), :] = jnp.sum(part1, axis=0, keepdims=True)
        sl[which, pl.ds(frames + f, 1), :] = jnp.sum(part2, axis=0, keepdims=True)

    for f in range(frames):
        loads[f].wait()

        def add_row(r, carry, f=f):
            one, two = frame_sums(fx[2 + f, 1 + r].astype(jnp.float32))
            return carry[0] + one, carry[1] + two

        zero = jnp.zeros((8, chans), jnp.float32)
        one, two = lax.fori_loop(0, rows, add_row, (zero, zero))
        put_sums(0, f, one, two)

    n_diag = (jnp.where(tm > 0, 1, 0) + jnp.where(tm < n_tm - 1, 1, 0)) * (
        jnp.where(rw > 0, 1, 0) + jnp.where(rw < n_rw - 1, 1, 0))
    pl.semaphore_wait(barrier, n_rw - 1 + n_tm - 1 + n_diag)

    def halo(buf, n, kind, e):
        def remote(src, dst, dev):
            return pltpu.make_async_remote_copy(
                src_ref=src, dst_ref=dst, send_sem=hsend.at[n, kind, e], recv_sem=hrecv.at[n, kind, e],
                device_id=dev, device_id_type=MESH)
        if kind == 0:
            return remote(buf.at[e, rows], buf.at[e, 0], (tm, rw + 1))
        if kind == 1:
            return remote(buf.at[e, 1], buf.at[e, rows + 1], (tm, rw - 1))
        if kind == 2:
            return remote(buf.at[e + frames, 1:rows + 1], buf.at[e, 1:rows + 1], (tm + 1, rw))
        if kind == 3:
            return remote(buf.at[e + frames, rows], buf.at[e, 0], (tm + 1, rw + 1))
        return remote(buf.at[e + frames, 1], buf.at[e, rows + 1], (tm + 1, rw - 1))

    sends = (rw < n_rw - 1, rw > 0, tm < n_tm - 1,
             (tm < n_tm - 1) & (rw < n_rw - 1), (tm < n_tm - 1) & (rw > 0))
    gets = (rw > 0, rw < n_rw - 1, tm > 0, (tm > 0) & (rw > 0), (tm > 0) & (rw < n_rw - 1))

    def halo_start(buf, n, kinds, e):
        for kind in kinds:
            @pl.when(sends[kind])
            def _():
                halo(buf, n, kind, e).start()

    def halo_sent(buf, n, kinds, e):
        for kind in kinds:
            @pl.when(sends[kind])
            def _():
                halo(buf, n, kind, e).wait_send()

    def halo_here(buf, n, kinds, e):
        for kind in kinds:
            @pl.when(gets[kind])
            def _():
                halo(buf, n, kind, e).wait_recv()

    def row_copy(n, k):
        return pltpu.make_async_remote_copy(
            src_ref=sl.at[n], dst_ref=ra.at[n, k - 1], send_sem=rsend.at[n, k - 1], recv_sem=rrecv.at[n, k - 1],
            device_id=(tm, lax.rem(rw + k, n_rw)), device_id_type=MESH)

    def time_copy(n, k):
        return pltpu.make_async_remote_copy(
            src_ref=sl.at[2 + n], dst_ref=tb.at[n, k - 1], send_sem=tsend.at[n, k - 1], recv_sem=trecv.at[n, k - 1],
            device_id=(tm + k, rw), device_id_type=MESH)

    def stats_start(n):
        for k in (4, 5, 3, 2, 6, 7, 1):
            row_copy(n, k).start()

    def stats_finish(n, gain, shift):
        for k in range(1, n_rw):
            row_copy(n, k).wait_recv()
        mine = sl[n] + jnp.sum(ra[n], axis=0)
        sl[2 + n] = mine
        for k in (10, 6, 9, 11, 14, 2, 5, 7, 8, 12, 13, 15, 3, 4, 1):
            @pl.when(tm + k < n_tm)
            def _():
                time_copy(n, k).start()
        for k in range(1, n_tm):
            @pl.when(tm >= k)
            def _():
                time_copy(n, k).wait_recv()
        far = jnp.sum(tb[n, 1:], axis=0)
        near = tb[n, 0]

        def running(lo):
            total = jnp.sum(far[lo:lo + frames], axis=0, keepdims=True)
            for f in range(frames - 1):
                total = total + near[lo + f:lo + f + 1]
            result = [total]
            total = total + near[lo + frames - 1:lo + frames]
            result.append(total)
            for f in range(frames):
                total = total + mine[lo + f:lo + f + 1]
                result.append(total)
            pad = jnp.zeros((8 - len(result), chans), jnp.float32)
            return group_sum(jnp.concatenate(result + [pad], axis=0), per_group)

        one, two = running(0), running(frames)
        place = lax.broadcasted_iota(jnp.int32, one.shape, 0)
        count = jnp.maximum(tm * frames + place - 1, 1).astype(jnp.float32) * float(n_rw * pix * per_group)
        mean = one / count
        var = two / count - mean * mean
        st[0] = mean
        st[1] = lax.rsqrt(var + EPSILON) * (0.5 * gain)
        st[2, 0:1] = 0.5 * shift

    def stats_sent(n):
        for k in range(1, n_rw):
            row_copy(n, k).wait_send()
        for k in range(1, n_tm):
            @pl.when(tm + k < n_tm)
            def _():
                time_copy(n, k).wait_send()

    def normalise(buf, e):
        mean, scale, shift = st[0, pl.ds(e, 1), :], st[1, pl.ds(e, 1), :], st[2, 0:1]

        def one(r):
            half = (buf[e, r].astype(jnp.float32) - mean) * scale + shift
            xn[e, pl.ds(pl.multiple_of(r * cols, cols), cols), :] = (half + half * jnp.tanh(half)).astype(jnp.bfloat16)

        def nothing(r):
            xn[e, pl.ds(r * cols, cols), :] = jnp.zeros((cols, chans), jnp.bfloat16)

        there = (tm > 0) | (e >= 2)

        @pl.when(there)
        def _():
            def two(i, _):
                one(1 + 2 * i)
                one(2 + 2 * i)
                return 0
            lax.fori_loop(0, rows // 2, two, 0)

        @pl.when(there & (rw > 0))
        def _():
            one(0)

        @pl.when(there & (rw < n_rw - 1))
        def _():
            one(rows + 1)

        @pl.when(jnp.logical_not(there))
        def _():
            xn[e] = jnp.zeros_like(xn[e])

        @pl.when(there & (rw == 0))
        def _():
            nothing(0)

        @pl.when(there & (rw == n_rw - 1))
        def _():
            nothing(rows + 1)

    col = lax.broadcasted_iota(jnp.int32, (pix, chans), 0) % cols

    def conv(w, f):
        total = None
        for a in range(3):
            for t in range(3):
                part = jnp.dot(xn[f + t, a * cols:a * cols + pix, :], w[a * 3 + t],
                               preferred_element_type=jnp.float32)
                total = part if total is None else total + part
        left = jnp.where(col == 0, 0.0, pltpu.roll(total[:, :chans], 1, 0))
        right = jnp.where(col == cols - 1, 0.0, pltpu.roll(total[:, 2 * chans:], pix - 1, 0))
        return total[:, chans:2 * chans] + left + right

    stats_start(0)
    for e in (1, 0):
        halo_start(fx, 0, (2, 3, 4), e)
    for e in range(2, 2 + frames):
        halo_start(fx, 0, (0, 1), e)
    for c in small:
        c.wait()
    stats_finish(0, par[0], par[1])
    for e in range(2, 2 + frames):
        halo_here(fx, 0, (0, 1), e)
        normalise(fx, e)
    for c in taps[:3]:
        c.wait()

    def first_conv(i, _):
        f = frames - 1 - i

        @pl.when(f < 2)
        def _():
            halo_here(fx, 0, (2, 3, 4), f)
            normalise(fx, f)

        y = (conv(wa, f) + par[2]).astype(jnp.bfloat16)
        bx[2 + f, 1:rows + 1] = y.reshape(rows, cols, chans)
        put_sums(1, f, *frame_sums(y.astype(jnp.float32)))
        halo_start(bx, 1, (0, 1), 2 + f)

        @pl.when(f >= frames - 2)
        def _():
            halo_start(bx, 1, (2, 3, 4), f + 2 - frames)
        return 0

    lax.fori_loop(0, frames, first_conv, 0)

    stats_start(1)
    stats_finish(1, par[3], par[4])
    for e in range(2, 2 + frames):
        halo_here(bx, 1, (0, 1), e)
        normalise(bx, e)
    for c in taps[3:]:
        c.wait()

    def out_copy(f):
        return pltpu.make_async_copy(ob.at[f], out.at[f], osem.at[f])

    def second_conv(i, _):
        f = frames - 1 - i

        @pl.when(f < 2)
        def _():
            halo_here(bx, 1, (2, 3, 4), f)
            normalise(bx, f)

        y = conv(wb, f) + par[5] + fx[2 + f, 1:rows + 1].reshape(pix, chans).astype(jnp.float32)
        ob[f] = y.astype(jnp.bfloat16).reshape(rows, cols, chans)
        out_copy(f).start()
        return 0

    lax.fori_loop(0, frames, second_conv, 0)

    for f in range(frames):
        out_copy(f).wait()
    for n, buf in enumerate((fx, bx)):
        for e in (1, 0):
            halo_sent(buf, n, (2, 3, 4), e)
        for e in range(2, 2 + frames):
            halo_sent(buf, n, (0, 1), e)
        stats_sent(n)


def solution(mesh):
    n_tm, n_rw = mesh.shape["tm"], mesh.shape["rows"]

    def on_device(features, gamma_one, beta_one, weight_one, bias_one, gamma_two, beta_two, weight_two, bias_two):
        frames, rows, cols, chans = features.shape
        taps = lambda w: w.reshape(9, 3, chans, chans)
        line = lambda v: v.reshape(1, chans)
        bf16, f32 = jnp.bfloat16, jnp.float32
        dma = pltpu.SemaphoreType.DMA
        return pl.pallas_call(
            functools.partial(block_kernel, n_tm, n_rw, frames, rows, cols, chans),
            out_shape=jax.ShapeDtypeStruct(features.shape, bf16),
            in_specs=[HBM] * 9,
            out_specs=HBM,
            scratch_shapes=[
                pltpu.VMEM((frames + 2, rows + 2, cols, chans), bf16),
                pltpu.VMEM((frames + 2, rows + 2, cols, chans), bf16),
                pltpu.VMEM((frames + 2, (rows + 2) * cols, chans), bf16),
                pltpu.VMEM((9, chans, 3 * chans), bf16),
                pltpu.VMEM((9, chans, 3 * chans), bf16),
                pltpu.VMEM(features.shape, bf16),
                pltpu.VMEM((6, 1, chans), f32),
                pltpu.VMEM((4, 2 * frames, chans), f32),
                pltpu.VMEM((2, n_rw - 1, 2 * frames, chans), f32),
                pltpu.VMEM((2, n_tm - 1, 2 * frames, chans), f32),
                pltpu.VMEM((3, 8, chans), f32),
                dma((frames,)), dma((6,)), dma((2, 3)), dma((frames,)),
                dma((2, n_rw - 1)), dma((2, n_rw - 1)), dma((2, n_tm - 1)), dma((2, n_tm - 1)),
                dma((2, 5, frames + 2)), dma((2, 5, frames + 2)),
            ],
            compiler_params=pltpu.CompilerParams(
                collective_id=0, has_side_effects=True, vmem_limit_bytes=48 << 20),
        )(features, line(gamma_one), line(beta_one), taps(weight_one), line(bias_one),
          line(gamma_two), line(beta_two), taps(weight_two), line(bias_two))

    placed = (P("tm", "rows", None, None), P(), P(), P(), P(), P(), P(), P(), P())
    return jax.shard_map(on_device, mesh=mesh, in_specs=placed, out_specs=P("tm", "rows", None, None), check_vma=False)
```

time: 257 us -> 79.7 us (0.31)
  the two profiles are of different devices: /device:TPU:3 before, /device:TPU:7 now
where the time goes in v1:
time: 79.7 us; the launch traced here: 79.5 us
  Pallas kernels  72.8 us (91%)
  local copies, waits for them, and re-layouts  6.62 us (8%)
    pallas_call x1, Pallas kernels, on_device(): pl.pallas_call(functools.partial(block_kernel, n_tm, n_rw, frames, rows,...  72.8 us
    unnamed x15, local copies, waits for them, and re-layouts  6.62 us

profile of v1, /device:TPU:7, one launch (start us, length us, event | category | flops | bytes accessed | tf_op | source)
XLA Modules:
  0.0 79.5 jit_solution(6185513775899648940)
XLA Ops:
  0.0 0.0 copy-start
  0.0 1.4 %copy-done = bf16[4,16,48,256]{3,2,1,0:T(8,128)(2,1)S(1)} copy-done((bf16[4,16,48,256]{3,2,1,0:T(8,128)(2,1)S(1)}, bf16[4,16,48,256]{3,2,1,0:T(8,128)(2,1)}, u32[]{:S(2)}) %copy-start) | copy-done | bytes 1572888
  1.4 0.0 copy-start.1
  1.4 0.7 copy-done.1
  2.1 0.0 copy-start.2
  2.1 0.7 copy-done.2
  2.8 0.0 copy-start.3
  2.8 0.7 copy-done.3
  3.4 0.0 copy-start.4
  3.4 0.7 copy-done.4
  4.1 0.0 copy-start.5
  4.1 0.7 copy-done.5
  4.8 0.0 copy-start.6
  4.8 0.7 copy-done.6
  5.5 72.8 %shard_map.91 = bf16[4,16,48,256]{3,2,1,0:T(8,128)(2,1)S(1)} custom-call(bf16[4,16,48,256]{3,2,1,0:T(8,128)(2,1)S(1)} %copy-done, f32[1,256]{1,0:T(1,128)S(1)} %bitcast.8, f32[1,256]{1,0:T(1,128)S(1)} %bitcast.9, bf16[9,3,256,256]{3,2,1,0:T(8,128)(2,1)} %bitcast.14, f32[1,256]{1,0:T(1,128)S(1)} %bitcast.10, f32[1,256]{1,0:T(1,128)S(1)} %bitcast.11, ...), custom_call_target="tpu_custom_call" | custom-call | tf_op jit(solution)/shard_map/pallas_call | solution.py:315
  78.3 1.1 %copy.11 = bf16[4,16,48,256]{3,2,1,0:T(8,128)(2,1)} copy(bf16[4,16,48,256]{3,2,1,0:T(8,128)(2,1)S(1)} %shard_map.91) | data formatting | bytes 3145728
Async XLA Ops:
  0.0 1.4 %copy-start = (bf16[4,16,48,256]{3,2,1,0:T(8,128)(2,1)S(1)}, bf16[4,16,48,256]{3,2,1,0:T(8,128)(2,1)}, u32[]{:S(2)}) copy-start(bf16[4,16,48,256]{3,2,1,0:T(8,128)(2,1)} %feat.1) | copy-start | bytes 4718596
  1.4 0.7 copy-start.1
  2.1 0.7 copy-start.2
  2.8 0.7 copy-start.3
  3.4 0.7 copy-start.4
  4.1 0.7 copy-start.5
  4.8 0.7 copy-start.6

commit v2 on v1

--- a/solution.py
+++ b/solution.py
@@ -83,6 +83,8 @@
         jnp.where(rw > 0, 1, 0) + jnp.where(rw < n_rw - 1, 1, 0))
     pl.semaphore_wait(barrier, n_rw - 1 + n_tm - 1 + n_diag)
 
+    quarter = rows // 4
+
     def halo(buf, n, kind, e):
         def remote(src, dst, dev):
             return pltpu.make_async_remote_copy(
@@ -93,14 +95,15 @@
         if kind == 1:
             return remote(buf.at[e, 1], buf.at[e, rows + 1], (tm, rw - 1))
         if kind == 2:
-            return remote(buf.at[e + frames, 1:rows + 1], buf.at[e, 1:rows + 1], (tm + 1, rw))
+            return remote(buf.at[e + frames, rows], buf.at[e, 0], (tm + 1, rw + 1))
         if kind == 3:
-            return remote(buf.at[e + frames, rows], buf.at[e, 0], (tm + 1, rw + 1))
-        return remote(buf.at[e + frames, 1], buf.at[e, rows + 1], (tm + 1, rw - 1))
-
-    sends = (rw < n_rw - 1, rw > 0, tm < n_tm - 1,
-             (tm < n_tm - 1) & (rw < n_rw - 1), (tm < n_tm - 1) & (rw > 0))
-    gets = (rw > 0, rw < n_rw - 1, tm > 0, (tm > 0) & (rw > 0), (tm > 0) & (rw < n_rw - 1))
+            return remote(buf.at[e + frames, 1], buf.at[e, rows + 1], (tm + 1, rw - 1))
+        part = pl.ds(1 + (kind - 4) * quarter, quarter)
+        return remote(buf.at[e + frames, part], buf.at[e, part], (tm + 1, rw))
+
+    ROW, TIME = (0, 1), (2, 3, 4, 5, 6, 7)
+    sends = (rw < n_rw - 1, rw > 0, (tm < n_tm - 1) & (rw < n_rw - 1), (tm < n_tm - 1) & (rw > 0)) + (tm < n_tm - 1,) * 4
+    gets = (rw > 0, rw < n_rw - 1, (tm > 0) & (rw > 0), (tm > 0) & (rw < n_rw - 1)) + (tm > 0,) * 4
 
     def halo_start(buf, n, kinds, e):
         for kind in kinds:
@@ -134,7 +137,7 @@
         for k in (4, 5, 3, 2, 6, 7, 1):
             row_copy(n, k).start()
 
-    def stats_finish(n, gain, shift):
+    def stats_finish(n, gain, shift, rest):
         for k in range(1, n_rw):
             row_copy(n, k).wait_recv()
         mine = sl[n] + jnp.sum(ra[n], axis=0)
@@ -143,6 +146,7 @@
             @pl.when(tm + k < n_tm)
             def _():
                 time_copy(n, k).start()
+        rest()
         for k in range(1, n_tm):
             @pl.when(tm >= k)
             def _():
@@ -234,15 +238,19 @@
         return total[:, chans:2 * chans] + left + right
 
     stats_start(0)
-    for e in (1, 0):
-        halo_start(fx, 0, (2, 3, 4), e)
     for e in range(2, 2 + frames):
-        halo_start(fx, 0, (0, 1), e)
+        halo_start(fx, 0, ROW, e)
+    halo_start(fx, 0, (4,), 1)
+
+    def rest_first():
+        halo_start(fx, 0, (5, 6, 7, 2, 3), 1)
+        halo_start(fx, 0, TIME, 0)
+
     for c in small:
         c.wait()
-    stats_finish(0, par[0], par[1])
+    stats_finish(0, par[0], par[1], rest_first)
     for e in range(2, 2 + frames):
-        halo_here(fx, 0, (0, 1), e)
+        halo_here(fx, 0, ROW, e)
         normalise(fx, e)
     for c in taps[:3]:
         c.wait()
@@ -252,25 +260,34 @@
 
         @pl.when(f < 2)
         def _():
-            halo_here(fx, 0, (2, 3, 4), f)
+            halo_here(fx, 0, TIME, f)
             normalise(fx, f)
 
         y = (conv(wa, f) + par[2]).astype(jnp.bfloat16)
         bx[2 + f, 1:rows + 1] = y.reshape(rows, cols, chans)
         put_sums(1, f, *frame_sums(y.astype(jnp.float32)))
-        halo_start(bx, 1, (0, 1), 2 + f)
-
-        @pl.when(f >= frames - 2)
-        def _():
-            halo_start(bx, 1, (2, 3, 4), f + 2 - frames)
+        halo_start(bx, 1, ROW, 2 + f)
+
+        @pl.when(i == 1)
+        def _():
+            halo_start(bx, 1, (4,), 1)
+
+        @pl.when(i == 2)
+        def _():
+            halo_start(bx, 1, (5,), 1)
         return 0
 
     lax.fori_loop(0, frames, first_conv, 0)
 
+    def rest_second():
+        halo_start(bx, 1, (7, 2, 3), 1)
+        halo_start(bx, 1, TIME, 0)
+
     stats_start(1)
-    stats_finish(1, par[3], par[4])
+    halo_start(bx, 1, (6,), 1)
+    stats_finish(1, par[3], par[4], rest_second)
     for e in range(2, 2 + frames):
-        halo_here(bx, 1, (0, 1), e)
+        halo_here(bx, 1, ROW, e)
         normalise(bx, e)
     for c in taps[3:]:
         c.wait()
@@ -283,7 +300,7 @@
 
         @pl.when(f < 2)
         def _():
-            halo_here(bx, 1, (2, 3, 4), f)
+            halo_here(bx, 1, TIME, f)
             normalise(bx, f)
 
         y = conv(wb, f) + par[5] + fx[2 + f, 1:rows + 1].reshape(pix, chans).astype(jnp.float32)
@@ -297,9 +314,9 @@
         out_copy(f).wait()
     for n, buf in enumerate((fx, bx)):
         for e in (1, 0):
-            halo_sent(buf, n, (2, 3, 4), e)
+            halo_sent(buf, n, TIME, e)
         for e in range(2, 2 + frames):
-            halo_sent(buf, n, (0, 1), e)
+            halo_sent(buf, n, ROW, e)
         stats_sent(n)
 
 
@@ -331,10 +348,10 @@
                 pltpu.VMEM((3, 8, chans), f32),
                 dma((frames,)), dma((6,)), dma((2, 3)), dma((frames,)),
                 dma((2, n_rw - 1)), dma((2, n_rw - 1)), dma((2, n_tm - 1)), dma((2, n_tm - 1)),
-                dma((2, 5, frames + 2)), dma((2, 5, frames + 2)),
+                dma((2, 8, frames + 2)), dma((2, 8, frames + 2)),
             ],
             compiler_params=pltpu.CompilerParams(
-                collective_id=0, has_side_effects=True, vmem_limit_bytes=48 << 20),
+                collective_id=0, has_side_effects=True, vmem_limit_bytes=64000 << 10),
         )(features, line(gamma_one), line(beta_one), taps(weight_one), line(bias_one),
           line(gamma_two), line(beta_two), taps(weight_two), line(bias_two))
 

time: 79.7 us -> 63.2 us (0.79)
  the two profiles are of different devices: /device:TPU:7 before, /device:TPU:3 now
where the time goes in v2:
time: 63.2 us; the launch traced here: 63.1 us
  Pallas kernels  60.4 us (96%)
  local copies, waits for them, and re-layouts  2.65 us (4%)
    pallas_call x1, Pallas kernels, on_device(): pl.pallas_call(functools.partial(block_kernel, n_tm, n_rw, frames, rows,...  60.4 us
    unnamed x1, local copies, waits for them, and re-layouts  2.65 us

profile of v2, /device:TPU:3, one launch (start us, length us, event | category | flops | bytes accessed | tf_op | source)
XLA Modules:
  0.0 63.1 jit_solution(2969371429223936957)
XLA Ops:
  0.0 60.4 %shard_map.91 = bf16[4,16,48,256]{3,2,1,0:T(8,128)(2,1)} custom-call(bf16[4,16,48,256]{3,2,1,0:T(8,128)(2,1)} %feat.1, f32[1,256]{1,0:T(1,128)} %bitcast.10, f32[1,256]{1,0:T(1,128)} %bitcast.11, bf16[9,3,256,256]{3,2,1,0:T(8,128)(2,1)} %bitcast.8, f32[1,256]{1,0:T(1,128)} %bitcast.12, f32[1,256]{1,0:T(1,128)} %bitcast.13, f32[1,256]{1,0:T(1,128)} %bitcast.14, ...), custom_call_target="tpu_custom_call" | custom-call | tf_op jit(solution)/shard_map/pallas_call | solution.py:332
  60.4 2.7 %copy.11 = bf16[4,16,48,256]{3,2,1,0:T(8,128)(2,1)} copy(bf16[4,16,48,256]{3,2,1,0:T(8,128)(2,1)} %shard_map.91) | data formatting | bytes 3145728

commit v3 on v2

--- a/solution.py
+++ b/solution.py
@@ -26,8 +26,8 @@
 
 def block_kernel(n_tm, n_rw, frames, rows, cols, chans,
                  feat, g1, b1, w1, c1, g2, b2, w2, c2, out,
-                 fx, bx, xn, wa, wb, ob, par, sl, ra, tb, st,
-                 lsem, psem, wsem, osem, rsend, rrecv, tsend, trecv, hsend, hrecv):
+                 fx, bx, xn, un, wa, wb, va, vb, par, sl, ra, tb, st,
+                 lsem, psem, wsem, rsend, rrecv, tsend, trecv, hsend, hrecv):
     tm = lax.axis_index("tm")
     rw = lax.axis_index("rows")
     pix = rows * cols
@@ -53,11 +53,6 @@
         pl.semaphore_signal(barrier, 1, device_id=(tm, lax.rem(rw + k, n_rw)), device_id_type=MESH)
     for k in range(1, n_tm):
         pl.semaphore_signal(barrier, 1, device_id=(lax.rem(tm + k, n_tm), rw), device_id_type=MESH)
-    for dt in (-1, 1):
-        for dr in (-1, 1):
-            @pl.when((tm + dt >= 0) & (tm + dt < n_tm) & (rw + dr >= 0) & (rw + dr < n_rw))
-            def _():
-                pl.semaphore_signal(barrier, 1, device_id=(tm + dt, rw + dr), device_id_type=MESH)
 
     def frame_sums(z):
         part1 = jnp.sum(z.reshape(z.shape[0] // 8, 8, chans), axis=0)
@@ -79,9 +74,7 @@
         one, two = lax.fori_loop(0, rows, add_row, (zero, zero))
         put_sums(0, f, one, two)
 
-    n_diag = (jnp.where(tm > 0, 1, 0) + jnp.where(tm < n_tm - 1, 1, 0)) * (
-        jnp.where(rw > 0, 1, 0) + jnp.where(rw < n_rw - 1, 1, 0))
-    pl.semaphore_wait(barrier, n_rw - 1 + n_tm - 1 + n_diag)
+    pl.semaphore_wait(barrier, n_rw - 1 + n_tm - 1)
 
     quarter = rows // 4
 
@@ -94,16 +87,12 @@
             return remote(buf.at[e, rows], buf.at[e, 0], (tm, rw + 1))
         if kind == 1:
             return remote(buf.at[e, 1], buf.at[e, rows + 1], (tm, rw - 1))
-        if kind == 2:
-            return remote(buf.at[e + frames, rows], buf.at[e, 0], (tm + 1, rw + 1))
-        if kind == 3:
-            return remote(buf.at[e + frames, 1], buf.at[e, rows + 1], (tm + 1, rw - 1))
-        part = pl.ds(1 + (kind - 4) * quarter, quarter)
+        part = pl.ds(1 + (kind - 2) * quarter, quarter)
         return remote(buf.at[e + frames, part], buf.at[e, part], (tm + 1, rw))
 
-    ROW, TIME = (0, 1), (2, 3, 4, 5, 6, 7)
-    sends = (rw < n_rw - 1, rw > 0, (tm < n_tm - 1) & (rw < n_rw - 1), (tm < n_tm - 1) & (rw > 0)) + (tm < n_tm - 1,) * 4
-    gets = (rw > 0, rw < n_rw - 1, (tm > 0) & (rw > 0), (tm > 0) & (rw < n_rw - 1)) + (tm > 0,) * 4
+    ROW, TIME, EDGES, MIDDLE = (0, 1), (2, 3, 4, 5), (2, 5), (3, 4)
+    sends = ((rw < n_rw - 1), (rw > 0)) + (tm < n_tm - 1,) * 4
+    gets = ((rw > 0), (rw < n_rw - 1)) + (tm > 0,) * 4
 
     def halo_start(buf, n, kinds, e):
         for kind in kinds:
@@ -122,6 +111,16 @@
             @pl.when(gets[kind])
             def _():
                 halo(buf, n, kind, e).wait_recv()
+
+    def halo_edge(buf, n, e):
+        @pl.when(tm > 0)
+        def _():
+            halo_start(buf, n, ROW, e)
+
+    def halo_corner(buf, n, e):
+        @pl.when(tm > 0)
+        def _():
+            halo_here(buf, n, ROW, e)
 
     def row_copy(n, k):
         return pltpu.make_async_remote_copy(
@@ -224,97 +223,138 @@
         def _():
             nothing(rows + 1)
 
+    def time_taps(w, v):
+        for a in range(3):
+            outer = (w[a * 3].astype(jnp.float32) + w[a * 3 + 2].astype(jnp.float32)) * 0.5
+            inner = w[a * 3 + 1].astype(jnp.float32) * 0.5
+            v[a] = (outer - inner).astype(jnp.bfloat16)
+            w[a * 3 + 1] = (outer + inner).astype(jnp.bfloat16)
+
+    def time_frames(f):
+        d0, d1, d2, d3 = [xn[f + i].astype(jnp.float32) for i in range(4)]
+        un[0] = (d0 - d2).astype(jnp.bfloat16)
+        un[1] = (d1 + d2).astype(jnp.bfloat16)
+        un[2] = (d2 - d1).astype(jnp.bfloat16)
+        un[3] = (d1 - d3).astype(jnp.bfloat16)
+
     col = lax.broadcasted_iota(jnp.int32, (pix, chans), 0) % cols
 
-    def conv(w, f):
-        total = None
-        for a in range(3):
-            for t in range(3):
-                part = jnp.dot(xn[f + t, a * cols:a * cols + pix, :], w[a * 3 + t],
-                               preferred_element_type=jnp.float32)
-                total = part if total is None else total + part
-        left = jnp.where(col == 0, 0.0, pltpu.roll(total[:, :chans], 1, 0))
-        right = jnp.where(col == cols - 1, 0.0, pltpu.roll(total[:, 2 * chans:], pix - 1, 0))
-        return total[:, chans:2 * chans] + left + right
+    def conv(w, v, bias):
+        outs = [None, None]
+        for e in (1, 0, 2):
+            m = []
+            for k in range(4):
+                total = None
+                for a in range(3):
+                    tap = (w.at[a * 3], w.at[a * 3 + 1], v.at[a], w.at[a * 3 + 2])[k]
+                    part = jnp.dot(un[k, a * cols:a * cols + pix, :], tap[:, e * chans:(e + 1) * chans],
+                                   preferred_element_type=jnp.float32)
+                    total = part if total is None else total + part
+                m.append(total)
+            pair = (m[0] + m[1] + m[2], m[1] - m[2] - m[3])
+            for i, y in enumerate(pair):
+                if e == 0:
+                    y = jnp.where(col == 0, 0.0, pltpu.roll(y, 1, 0))
+                if e == 2:
+                    y = jnp.where(col == cols - 1, 0.0, pltpu.roll(y, pix - 1, 0))
+                outs[i] = y + bias if outs[i] is None else outs[i] + y
+        return outs
 
     stats_start(0)
     for e in range(2, 2 + frames):
         halo_start(fx, 0, ROW, e)
-    halo_start(fx, 0, (4,), 1)
-
-    def rest_first():
-        halo_start(fx, 0, (5, 6, 7, 2, 3), 1)
-        halo_start(fx, 0, TIME, 0)
-
+    halo_start(fx, 0, EDGES[:1], 1)
     for c in small:
         c.wait()
+    for c in taps[:3]:
+        c.wait()
+    time_taps(wa, va)
+
+    def rest_first():
+        halo_start(fx, 0, EDGES[1:], 1)
+        halo_start(fx, 0, EDGES, 0)
+        halo_start(fx, 0, MIDDLE, 1)
+        halo_start(fx, 0, MIDDLE, 0)
+        for c in taps[3:]:
+            c.wait()
+        time_taps(wb, vb)
+
+    def edges_on(buf, n):
+        for e in (1, 0):
+            halo_here(buf, n, EDGES, e)
+            halo_edge(buf, n, e)
+
     stats_finish(0, par[0], par[1], rest_first)
     for e in range(2, 2 + frames):
         halo_here(fx, 0, ROW, e)
         normalise(fx, e)
-    for c in taps[:3]:
-        c.wait()
 
     def first_conv(i, _):
-        f = frames - 1 - i
-
-        @pl.when(f < 2)
-        def _():
-            halo_here(fx, 0, TIME, f)
-            normalise(fx, f)
-
-        y = (conv(wa, f) + par[2]).astype(jnp.bfloat16)
-        bx[2 + f, 1:rows + 1] = y.reshape(rows, cols, chans)
-        put_sums(1, f, *frame_sums(y.astype(jnp.float32)))
-        halo_start(bx, 1, ROW, 2 + f)
+        f = 2 - 2 * i
 
         @pl.when(i == 1)
         def _():
-            halo_start(bx, 1, (4,), 1)
-
-        @pl.when(i == 2)
-        def _():
-            halo_start(bx, 1, (5,), 1)
+            edges_on(fx, 0)
+            for e in (1, 0):
+                halo_here(fx, 0, MIDDLE, e)
+                halo_corner(fx, 0, e)
+                normalise(fx, e)
+
+        time_frames(f)
+        for o, y in enumerate(conv(wa, va, par[2])):
+            y = y.astype(jnp.bfloat16)
+            bx[2 + f + o, 1:rows + 1] = y.reshape(rows, cols, chans)
+            put_sums(1, f + o, *frame_sums(y.astype(jnp.float32)))
+
+        @pl.when(i == 0)
+        def _():
+            for e in (4, 5):
+                halo_start(bx, 1, ROW, e)
+            halo_start(bx, 1, EDGES, 1)
         return 0
 
-    lax.fori_loop(0, frames, first_conv, 0)
+    lax.fori_loop(0, 2, first_conv, 0)
 
     def rest_second():
-        halo_start(bx, 1, (7, 2, 3), 1)
-        halo_start(bx, 1, TIME, 0)
+        halo_start(bx, 1, EDGES[1:], 0)
+        halo_start(bx, 1, MIDDLE, 1)
+        halo_start(bx, 1, MIDDLE, 0)
 
     stats_start(1)
-    halo_start(bx, 1, (6,), 1)
+    for e in (2, 3):
+        halo_start(bx, 1, ROW, e)
+    halo_start(bx, 1, EDGES[:1], 0)
     stats_finish(1, par[3], par[4], rest_second)
     for e in range(2, 2 + frames):
         halo_here(bx, 1, ROW, e)
         normalise(bx, e)
-    for c in taps[3:]:
-        c.wait()
-
-    def out_copy(f):
-        return pltpu.make_async_copy(ob.at[f], out.at[f], osem.at[f])
 
     def second_conv(i, _):
-        f = frames - 1 - i
-
-        @pl.when(f < 2)
-        def _():
-            halo_here(bx, 1, TIME, f)
-            normalise(bx, f)
-
-        y = conv(wb, f) + par[5] + fx[2 + f, 1:rows + 1].reshape(pix, chans).astype(jnp.float32)
-        ob[f] = y.astype(jnp.bfloat16).reshape(rows, cols, chans)
-        out_copy(f).start()
+        f = 2 - 2 * i
+
+        @pl.when(i == 1)
+        def _():
+            edges_on(bx, 1)
+            for e in (1, 0):
+                halo_here(bx, 1, MIDDLE, e)
+                halo_corner(bx, 1, e)
+                normalise(bx, e)
+
+        time_frames(f)
+        for o, y in enumerate(conv(wb, vb, par[5])):
+            y = y + fx[2 + f + o, 1:rows + 1].reshape(pix, chans).astype(jnp.float32)
+            out[f + o] = y.astype(jnp.bfloat16).reshape(rows, cols, chans)
         return 0
 
-    lax.fori_loop(0, frames, second_conv, 0)
-
-    for f in range(frames):
-        out_copy(f).wait()
+    lax.fori_loop(0, 2, second_conv, 0)
+
     for n, buf in enumerate((fx, bx)):
         for e in (1, 0):
             halo_sent(buf, n, TIME, e)
+
+            @pl.when(tm > 0)
+            def _():
+                halo_sent(buf, n, ROW, e)
         for e in range(2, 2 + frames):
             halo_sent(buf, n, ROW, e)
         stats_sent(n)
@@ -333,27 +373,30 @@
             functools.partial(block_kernel, n_tm, n_rw, frames, rows, cols, chans),
             out_shape=jax.ShapeDtypeStruct(features.shape, bf16),
             in_specs=[HBM] * 9,
-            out_specs=HBM,
+            out_specs=pl.BlockSpec(memory_space=pltpu.VMEM),
             scratch_shapes=[
                 pltpu.VMEM((frames + 2, rows + 2, cols, chans), bf16),
                 pltpu.VMEM((frames + 2, rows + 2, cols, chans), bf16),
                 pltpu.VMEM((frames + 2, (rows + 2) * cols, chans), bf16),
+                pltpu.VMEM((4, (rows + 2) * cols, chans), bf16),
                 pltpu.VMEM((9, chans, 3 * chans), bf16),
                 pltpu.VMEM((9, chans, 3 * chans), bf16),
-                pltpu.VMEM(features.shape, bf16),
+                pltpu.VMEM((3, chans, 3 * chans), bf16),
+                pltpu.VMEM((3, chans, 3 * chans), bf16),
                 pltpu.VMEM((6, 1, chans), f32),
                 pltpu.VMEM((4, 2 * frames, chans), f32),
                 pltpu.VMEM((2, n_rw - 1, 2 * frames, chans), f32),
                 pltpu.VMEM((2, n_tm - 1, 2 * frames, chans), f32),
                 pltpu.VMEM((3, 8, chans), f32),
-                dma((frames,)), dma((6,)), dma((2, 3)), dma((frames,)),
+                dma((frames,)), dma((6,)), dma((2, 3)),
                 dma((2, n_rw - 1)), dma((2, n_rw - 1)), dma((2, n_tm - 1)), dma((2, n_tm - 1)),
-                dma((2, 8, frames + 2)), dma((2, 8, frames + 2)),
+                dma((2, 6, frames + 2)), dma((2, 6, frames + 2)),
             ],
             compiler_params=pltpu.CompilerParams(
-                collective_id=0, has_side_effects=True, vmem_limit_bytes=64000 << 10),
-        )(features, line(gamma_one), line(beta_one), taps(weight_one), line(bias_one),
-          line(gamma_two), line(beta_two), taps(weight_two), line(bias_two))
+                collective_id=0, has_side_effects=True, vmem_limit_bytes=52 << 20),
+        )(*[pltpu.with_memory_space_constraint(v, pltpu.HBM) for v in (
+            features, line(gamma_one), line(beta_one), taps(weight_one), line(bias_one),
+            line(gamma_two), line(beta_two), taps(weight_two), line(bias_two))])
 
     placed = (P("tm", "rows", None, None), P(), P(), P(), P(), P(), P(), P(), P())
     return jax.shard_map(on_device, mesh=mesh, in_specs=placed, out_specs=P("tm", "rows", None, None), check_vma=False)

time: 63.2 us -> 58.9 us (0.932)
  Pallas kernels: 60.4 us -> 57.4 us
  local copies, waits for them, and re-layouts: 2.65 us -> 1.15 us
    pallas_call x1, Pallas kernels: 60.4 us -> 57.4 us  [on_device(): pl.pallas_call(functools.partial(block_kernel, n_tm, n_rw, frames, rows,...]
    unnamed x1, local copies, waits for them, and re-layouts: 2.65 us -> 1.15 us
where the time goes in v3:
time: 58.9 us; the launch traced here: 58.5 us
  Pallas kernels  57.4 us (97%)
  local copies, waits for them, and re-layouts  1.15 us (2%)
    pallas_call x1, Pallas kernels, on_device(): pl.pallas_call(functools.partial(block_kernel, n_tm, n_rw, frames, rows,...  57.4 us

profile of v3, /device:TPU:3, one launch (start us, length us, event | category | flops | bytes accessed | tf_op | source)
XLA Modules:
  0.0 58.5 jit_solution(6430467929173774206)
XLA Ops:
  0.0 57.4 %shard_map.91 = bf16[4,16,48,256]{3,2,1,0:T(8,128)(2,1)S(1)} custom-call(bf16[4,16,48,256]{3,2,1,0:T(8,128)(2,1)} %feat.1, f32[1,256]{1,0:T(1,128)} %bitcast.10, f32[1,256]{1,0:T(1,128)} %bitcast.11, bf16[9,3,256,256]{3,2,1,0:T(8,128)(2,1)} %bitcast.8, f32[1,256]{1,0:T(1,128)} %bitcast.12, f32[1,256]{1,0:T(1,128)} %bitcast.13, f32[1,256]{1,0:T(1,128)} %bitcast.14, ...), custom_call_target="tpu_custom_call" | custom-call | tf_op jit(solution)/shard_map/pallas_call | solution.py:372
  57.4 1.1 %copy.11 = bf16[4,16,48,256]{3,2,1,0:T(8,128)(2,1)} copy(bf16[4,16,48,256]{3,2,1,0:T(8,128)(2,1)S(1)} %shard_map.91) | data formatting | bytes 3145728

commit v4 on v3

--- a/solution.py
+++ b/solution.py
@@ -26,7 +26,7 @@
 
 def block_kernel(n_tm, n_rw, frames, rows, cols, chans,
                  feat, g1, b1, w1, c1, g2, b2, w2, c2, out,
-                 fx, bx, xn, un, wa, wb, va, vb, par, sl, ra, tb, st,
+                 fx, bx, xn, un, acc, wa, wb, va, vb, par, sl, ln, ra, tb, st,
                  lsem, psem, wsem, rsend, rrecv, tsend, trecv, hsend, hrecv):
     tm = lax.axis_index("tm")
     rw = lax.axis_index("rows")
@@ -67,11 +67,11 @@
         loads[f].wait()
 
         def add_row(r, carry, f=f):
-            one, two = frame_sums(fx[2 + f, 1 + r].astype(jnp.float32))
+            one, two = frame_sums(fx[2 + f, pl.ds(1 + 4 * r, 4)].reshape(4 * cols, chans).astype(jnp.float32))
             return carry[0] + one, carry[1] + two
 
         zero = jnp.zeros((8, chans), jnp.float32)
-        one, two = lax.fori_loop(0, rows, add_row, (zero, zero))
+        one, two = lax.fori_loop(0, rows // 4, add_row, (zero, zero))
         put_sums(0, f, one, two)
 
     pl.semaphore_wait(barrier, n_rw - 1 + n_tm - 1)
@@ -122,25 +122,35 @@
         def _():
             halo_here(buf, n, ROW, e)
 
+    place = lax.broadcasted_iota(jnp.int32, (2 * frames, chans), 0)
+    keep = (lax.broadcasted_iota(jnp.int32, (2 * frames, chans), 1) % per_group) == place
+
+    def pack(x):
+        return jnp.sum(jnp.where(keep, group_sum(x, per_group), 0.0), axis=0, keepdims=True)
+
+    def unpack(line):
+        return group_sum(jnp.where(keep, line, 0.0), per_group)
+
     def row_copy(n, k):
         return pltpu.make_async_remote_copy(
-            src_ref=sl.at[n], dst_ref=ra.at[n, k - 1], send_sem=rsend.at[n, k - 1], recv_sem=rrecv.at[n, k - 1],
+            src_ref=ln.at[n], dst_ref=ra.at[n, k - 1], send_sem=rsend.at[n, k - 1], recv_sem=rrecv.at[n, k - 1],
             device_id=(tm, lax.rem(rw + k, n_rw)), device_id_type=MESH)
 
     def time_copy(n, k):
         return pltpu.make_async_remote_copy(
-            src_ref=sl.at[2 + n], dst_ref=tb.at[n, k - 1], send_sem=tsend.at[n, k - 1], recv_sem=trecv.at[n, k - 1],
+            src_ref=ln.at[2 + n], dst_ref=tb.at[n, k - 1], send_sem=tsend.at[n, k - 1], recv_sem=trecv.at[n, k - 1],
             device_id=(tm + k, rw), device_id_type=MESH)
 
     def stats_start(n):
+        ln[n] = pack(sl[n])
         for k in (4, 5, 3, 2, 6, 7, 1):
             row_copy(n, k).start()
 
     def stats_finish(n, gain, shift, rest):
         for k in range(1, n_rw):
             row_copy(n, k).wait_recv()
-        mine = sl[n] + jnp.sum(ra[n], axis=0)
-        sl[2 + n] = mine
+        line = ln[n] + jnp.sum(ra[n], axis=0)
+        ln[2 + n] = line
         for k in (10, 6, 9, 11, 14, 2, 5, 7, 8, 12, 13, 15, 3, 4, 1):
             @pl.when(tm + k < n_tm)
             def _():
@@ -150,8 +160,7 @@
             @pl.when(tm >= k)
             def _():
                 time_copy(n, k).wait_recv()
-        far = jnp.sum(tb[n, 1:], axis=0)
-        near = tb[n, 0]
+        far, near, mine = unpack(jnp.sum(tb[n, 1:], axis=0)), unpack(tb[n, 0]), unpack(line)
 
         def running(lo):
             total = jnp.sum(far[lo:lo + frames], axis=0, keepdims=True)
@@ -164,10 +173,9 @@
                 total = total + mine[lo + f:lo + f + 1]
                 result.append(total)
             pad = jnp.zeros((8 - len(result), chans), jnp.float32)
-            return group_sum(jnp.concatenate(result + [pad], axis=0), per_group)
+            return jnp.concatenate(result + [pad], axis=0)
 
         one, two = running(0), running(frames)
-        place = lax.broadcasted_iota(jnp.int32, one.shape, 0)
         count = jnp.maximum(tm * frames + place - 1, 1).astype(jnp.float32) * float(n_rw * pix * per_group)
         mean = one / count
         var = two / count - mean * mean
@@ -197,11 +205,11 @@
 
         @pl.when(there)
         def _():
-            def two(i, _):
-                one(1 + 2 * i)
-                one(2 + 2 * i)
+            def four(i, _):
+                for r in range(1, 5):
+                    one(r + 4 * i)
                 return 0
-            lax.fori_loop(0, rows // 2, two, 0)
+            lax.fori_loop(0, rows // 4, four, 0)
 
         @pl.when(there & (rw > 0))
         def _():
@@ -230,35 +238,45 @@
             v[a] = (outer - inner).astype(jnp.bfloat16)
             w[a * 3 + 1] = (outer + inner).astype(jnp.bfloat16)
 
-    def time_frames(f):
-        d0, d1, d2, d3 = [xn[f + i].astype(jnp.float32) for i in range(4)]
-        un[0] = (d0 - d2).astype(jnp.bfloat16)
+    def frame(e):
+        return xn[e].astype(jnp.float32)
+
+    col = lax.broadcasted_iota(jnp.int32, (pix, chans), 0) % cols
+
+    def product(w, v, k, e):
+        total = None
+        for a in range(3):
+            tap = (w.at[a * 3], w.at[a * 3 + 1], v.at[a], w.at[a * 3 + 2])[k]
+            part = jnp.dot(un[k, a * cols:a * cols + pix, :], tap[:, e * chans:(e + 1) * chans],
+                           preferred_element_type=jnp.float32)
+            total = part if total is None else total + part
+        return total
+
+    def column(y, e):
+        if e == 0:
+            return jnp.where(col == 0, 0.0, pltpu.roll(y, 1, 0))
+        if e == 2:
+            return jnp.where(col == cols - 1, 0.0, pltpu.roll(y, pix - 1, 0))
+        return y
+
+    def conv_late(w, v, f, bias):
+        d1, d2, d3 = frame(f + 1), frame(f + 2), frame(f + 3)
         un[1] = (d1 + d2).astype(jnp.bfloat16)
         un[2] = (d2 - d1).astype(jnp.bfloat16)
         un[3] = (d1 - d3).astype(jnp.bfloat16)
-
-    col = lax.broadcasted_iota(jnp.int32, (pix, chans), 0) % cols
-
-    def conv(w, v, bias):
-        outs = [None, None]
+        y0 = y1 = bias
         for e in (1, 0, 2):
-            m = []
-            for k in range(4):
-                total = None
-                for a in range(3):
-                    tap = (w.at[a * 3], w.at[a * 3 + 1], v.at[a], w.at[a * 3 + 2])[k]
-                    part = jnp.dot(un[k, a * cols:a * cols + pix, :], tap[:, e * chans:(e + 1) * chans],
-                                   preferred_element_type=jnp.float32)
-                    total = part if total is None else total + part
-                m.append(total)
-            pair = (m[0] + m[1] + m[2], m[1] - m[2] - m[3])
-            for i, y in enumerate(pair):
-                if e == 0:
-                    y = jnp.where(col == 0, 0.0, pltpu.roll(y, 1, 0))
-                if e == 2:
-                    y = jnp.where(col == cols - 1, 0.0, pltpu.roll(y, pix - 1, 0))
-                outs[i] = y + bias if outs[i] is None else outs[i] + y
-        return outs
+            m1, m2, m3 = [product(w, v, k, e) for k in (1, 2, 3)]
+            y0, y1 = y0 + column(m1 + m2, e), y1 + column(m1 - m2 - m3, e)
+        acc[...] = y0
+        return y1
+
+    def conv_early(w, v, f):
+        un[0] = (frame(f) - frame(f + 2)).astype(jnp.bfloat16)
+        y = acc[...]
+        for e in (1, 0, 2):
+            y = y + column(product(w, v, 0, e), e)
+        return y
 
     stats_start(0)
     for e in range(2, 2 + frames):
@@ -273,8 +291,7 @@
     def rest_first():
         halo_start(fx, 0, EDGES[1:], 1)
         halo_start(fx, 0, EDGES, 0)
-        halo_start(fx, 0, MIDDLE, 1)
-        halo_start(fx, 0, MIDDLE, 0)
+        halo_start(fx, 0, MIDDLE[:1], 1)
         for c in taps[3:]:
             c.wait()
         time_taps(wb, vb)
@@ -288,43 +305,49 @@
     for e in range(2, 2 + frames):
         halo_here(fx, 0, ROW, e)
         normalise(fx, e)
+    edges_on(fx, 0)
+    halo_start(fx, 0, MIDDLE[1:], 1)
+    halo_start(fx, 0, MIDDLE, 0)
+
+    def earlier(buf, n, i, e):
+        @pl.when(i == 1)
+        def _():
+            halo_here(buf, n, MIDDLE, e)
+            halo_corner(buf, n, e)
+            normalise(buf, e)
 
     def first_conv(i, _):
         f = 2 - 2 * i
 
-        @pl.when(i == 1)
-        def _():
-            edges_on(fx, 0)
-            for e in (1, 0):
-                halo_here(fx, 0, MIDDLE, e)
-                halo_corner(fx, 0, e)
-                normalise(fx, e)
-
-        time_frames(f)
-        for o, y in enumerate(conv(wa, va, par[2])):
+        def put(g, y):
             y = y.astype(jnp.bfloat16)
-            bx[2 + f + o, 1:rows + 1] = y.reshape(rows, cols, chans)
-            put_sums(1, f + o, *frame_sums(y.astype(jnp.float32)))
+            bx[2 + g, 1:rows + 1] = y.reshape(rows, cols, chans)
+            put_sums(1, g, *frame_sums(y.astype(jnp.float32)))
+            halo_start(bx, 1, ROW, 2 + g)
+
+        earlier(fx, 0, i, 1)
+        put(f + 1, conv_late(wa, va, f, par[2]))
 
         @pl.when(i == 0)
         def _():
-            for e in (4, 5):
-                halo_start(bx, 1, ROW, e)
             halo_start(bx, 1, EDGES, 1)
+
+        earlier(fx, 0, i, 0)
+        put(f, conv_early(wa, va, f))
         return 0
 
     lax.fori_loop(0, 2, first_conv, 0)
 
     def rest_second():
         halo_start(bx, 1, EDGES[1:], 0)
-        halo_start(bx, 1, MIDDLE, 1)
-        halo_start(bx, 1, MIDDLE, 0)
+        halo_start(bx, 1, MIDDLE[:1], 1)
 
     stats_start(1)
-    for e in (2, 3):
-        halo_start(bx, 1, ROW, e)
     halo_start(bx, 1, EDGES[:1], 0)
     stats_finish(1, par[3], par[4], rest_second)
+    edges_on(bx, 1)
+    halo_start(bx, 1, MIDDLE[1:], 1)
+    halo_start(bx, 1, MIDDLE, 0)
     for e in range(2, 2 + frames):
         halo_here(bx, 1, ROW, e)
         normalise(bx, e)
@@ -332,18 +355,14 @@
     def second_conv(i, _):
         f = 2 - 2 * i
 
-        @pl.when(i == 1)
-        def _():
-            edges_on(bx, 1)
-            for e in (1, 0):
-                halo_here(bx, 1, MIDDLE, e)
-                halo_corner(bx, 1, e)
-                normalise(bx, e)
-
-        time_frames(f)
-        for o, y in enumerate(conv(wb, vb, par[5])):
-            y = y + fx[2 + f + o, 1:rows + 1].reshape(pix, chans).astype(jnp.float32)
-            out[f + o] = y.astype(jnp.bfloat16).reshape(rows, cols, chans)
+        def put(g, y):
+            y = y + fx[2 + g, 1:rows + 1].reshape(pix, chans).astype(jnp.float32)
+            out[g] = y.astype(jnp.bfloat16).reshape(rows, cols, chans)
+
+        earlier(bx, 1, i, 1)
+        put(f + 1, conv_late(wb, vb, f, par[5]))
+        earlier(bx, 1, i, 0)
+        put(f, conv_early(wb, vb, f))
         return 0
 
     lax.fori_loop(0, 2, second_conv, 0)
@@ -379,14 +398,16 @@
                 pltpu.VMEM((frames + 2, rows + 2, cols, chans), bf16),
                 pltpu.VMEM((frames + 2, (rows + 2) * cols, chans), bf16),
                 pltpu.VMEM((4, (rows + 2) * cols, chans), bf16),
+                pltpu.VMEM((rows * cols, chans), f32),
                 pltpu.VMEM((9, chans, 3 * chans), bf16),
                 pltpu.VMEM((9, chans, 3 * chans), bf16),
                 pltpu.VMEM((3, chans, 3 * chans), bf16),
                 pltpu.VMEM((3, chans, 3 * chans), bf16),
                 pltpu.VMEM((6, 1, chans), f32),
-                pltpu.VMEM((4, 2 * frames, chans), f32),
-                pltpu.VMEM((2, n_rw - 1, 2 * frames, chans), f32),
-                pltpu.VMEM((2, n_tm - 1, 2 * frames, chans), f32),
+                pltpu.VMEM((2, 2 * frames, chans), f32),
+                pltpu.VMEM((4, 1, chans), f32),
+                pltpu.VMEM((2, n_rw - 1, 1, chans), f32),
+                pltpu.VMEM((2, n_tm - 1, 1, chans), f32),
                 pltpu.VMEM((3, 8, chans), f32),
                 dma((frames,)), dma((6,)), dma((2, 3)),
                 dma((2, n_rw - 1)), dma((2, n_rw - 1)), dma((2, n_tm - 1)), dma((2, n_tm - 1)),

time: 58.9 us -> 54.6 us (0.927)
  Pallas kernels: 57.4 us -> 52.8 us
    pallas_call x1, Pallas kernels: 57.4 us -> 52.8 us  [on_device(): pl.pallas_call(functools.partial(block_kernel, n_tm, n_rw, frames, rows,...]
where the time goes in v4:
time: 54.6 us; the launch traced here: 54 us
  Pallas kernels  52.8 us (97%)
  local copies, waits for them, and re-layouts  1.15 us (2%)
    pallas_call x1, Pallas kernels, on_device(): pl.pallas_call(functools.partial(block_kernel, n_tm, n_rw, frames, rows,...  52.8 us
    unnamed x1, local copies, waits for them, and re-layouts  1.15 us

profile of v4, /device:TPU:3, one launch (start us, length us, event | category | flops | bytes accessed | tf_op | source)
XLA Modules:
  0.0 54.0 jit_solution(11109158031701498436)
XLA Ops:
  0.0 52.8 %shard_map.91 = bf16[4,16,48,256]{3,2,1,0:T(8,128)(2,1)S(1)} custom-call(bf16[4,16,48,256]{3,2,1,0:T(8,128)(2,1)} %feat.1, f32[1,256]{1,0:T(1,128)} %bitcast.10, f32[1,256]{1,0:T(1,128)} %bitcast.11, bf16[9,3,256,256]{3,2,1,0:T(8,128)(2,1)} %bitcast.8, f32[1,256]{1,0:T(1,128)} %bitcast.12, f32[1,256]{1,0:T(1,128)} %bitcast.13, f32[1,256]{1,0:T(1,128)} %bitcast.14, ...), custom_call_target="tpu_custom_call" | custom-call | tf_op jit(solution)/shard_map/pallas_call | solution.py:391
  52.8 1.1 %copy.11 = bf16[4,16,48,256]{3,2,1,0:T(8,128)(2,1)} copy(bf16[4,16,48,256]{3,2,1,0:T(8,128)(2,1)S(1)} %shard_map.91) | data formatting | bytes 3145728

commit v5 on v4

--- a/solution.py
+++ b/solution.py
@@ -10,6 +10,7 @@
 MESH = pl.DeviceIdType.MESH
 GROUPS = 32
 EPSILON = 1e-06
+RING = 4
 HBM = pl.BlockSpec(memory_space=pltpu.HBM)
 
 
@@ -26,8 +27,8 @@
 
 def block_kernel(n_tm, n_rw, frames, rows, cols, chans,
                  feat, g1, b1, w1, c1, g2, b2, w2, c2, out,
-                 fx, bx, xn, un, acc, wa, wb, va, vb, par, sl, ln, ra, tb, st,
-                 lsem, psem, wsem, rsend, rrecv, tsend, trecv, hsend, hrecv):
+                 fx, bx, xn, un, acc, wa, wb, va, vb, par, sl, ln, ra, tb, st, rel,
+                 lsem, psem, wsem, rsend, rrecv, tsend, trecv, hsend, hrecv, gsend, grecv):
     tm = lax.axis_index("tm")
     rw = lax.axis_index("rows")
     pix = rows * cols
@@ -112,6 +113,34 @@
             def _():
                 halo(buf, n, kind, e).wait_recv()
 
+    LONG = ((4, 0), (4, 1))
+
+    def ring(step):
+        return tm - lax.rem(tm, RING) + lax.rem(tm + step, RING)
+
+    def long_copy(buf, n, hop):
+        kind, e = LONG[n]
+        part = pl.ds(1 + (kind - 2) * quarter, quarter)
+        src = (buf.at[e + frames, part], rel.at[n, 0], rel.at[n, 1])[hop]
+        dst = (rel.at[n, 0], rel.at[n, 1], buf.at[e, part])[hop]
+        return pltpu.make_async_remote_copy(
+            src_ref=src, dst_ref=dst, send_sem=gsend.at[n, hop],
+            recv_sem=hrecv.at[n, kind, e] if hop == 2 else grecv.at[n, hop],
+            device_id=(ring(2) + 1 if hop == 2 else ring(RING - 1), rw), device_id_type=MESH)
+
+    def long_start(buf, n, hop):
+        @pl.when(ring(hop) < n_tm - 1)
+        def _():
+            if hop:
+                long_copy(buf, n, hop - 1).wait_recv()
+            long_copy(buf, n, hop).start()
+
+    def long_sent(buf, n):
+        for hop in range(3):
+            @pl.when(ring(hop) < n_tm - 1)
+            def _():
+                long_copy(buf, n, hop).wait_send()
+
     def halo_edge(buf, n, e):
         @pl.when(tm > 0)
         def _():
@@ -281,7 +310,9 @@
     stats_start(0)
     for e in range(2, 2 + frames):
         halo_start(fx, 0, ROW, e)
-    halo_start(fx, 0, EDGES[:1], 1)
+    halo_start(fx, 0, EDGES, 1)
+    halo_start(fx, 0, EDGES[:1], 0)
+    long_start(fx, 0, 0)
     for c in small:
         c.wait()
     for c in taps[:3]:
@@ -289,12 +320,12 @@
     time_taps(wa, va)
 
     def rest_first():
-        halo_start(fx, 0, EDGES[1:], 1)
-        halo_start(fx, 0, EDGES, 0)
-        halo_start(fx, 0, MIDDLE[:1], 1)
+        halo_start(fx, 0, EDGES[1:], 0)
+        halo_start(fx, 0, MIDDLE, 1)
         for c in taps[3:]:
             c.wait()
         time_taps(wb, vb)
+        long_start(fx, 0, 1)
 
     def edges_on(buf, n):
         for e in (1, 0):
@@ -306,8 +337,8 @@
         halo_here(fx, 0, ROW, e)
         normalise(fx, e)
     edges_on(fx, 0)
-    halo_start(fx, 0, MIDDLE[1:], 1)
-    halo_start(fx, 0, MIDDLE, 0)
+    halo_start(fx, 0, MIDDLE[:1], 0)
+    long_start(fx, 0, 2)
 
     def earlier(buf, n, i, e):
         @pl.when(i == 1)
@@ -331,6 +362,11 @@
         @pl.when(i == 0)
         def _():
             halo_start(bx, 1, EDGES, 1)
+            long_start(bx, 1, 0)
+
+        @pl.when(i == 1)
+        def _():
+            long_start(bx, 1, 1)
 
         earlier(fx, 0, i, 0)
         put(f, conv_early(wa, va, f))
@@ -341,12 +377,12 @@
     def rest_second():
         halo_start(bx, 1, EDGES[1:], 0)
         halo_start(bx, 1, MIDDLE[:1], 1)
+        long_start(bx, 1, 2)
 
     stats_start(1)
     halo_start(bx, 1, EDGES[:1], 0)
     stats_finish(1, par[3], par[4], rest_second)
     edges_on(bx, 1)
-    halo_start(bx, 1, MIDDLE[1:], 1)
     halo_start(bx, 1, MIDDLE, 0)
     for e in range(2, 2 + frames):
         halo_here(bx, 1, ROW, e)
@@ -369,7 +405,7 @@
 
     for n, buf in enumerate((fx, bx)):
         for e in (1, 0):
-            halo_sent(buf, n, TIME, e)
+            halo_sent(buf, n, [kind for kind in TIME if (kind, e) != LONG[n]], e)
 
             @pl.when(tm > 0)
             def _():
@@ -377,6 +413,7 @@
         for e in range(2, 2 + frames):
             halo_sent(buf, n, ROW, e)
         stats_sent(n)
+        long_sent(buf, n)
 
 
 def solution(mesh):
@@ -409,9 +446,10 @@
                 pltpu.VMEM((2, n_rw - 1, 1, chans), f32),
                 pltpu.VMEM((2, n_tm - 1, 1, chans), f32),
                 pltpu.VMEM((3, 8, chans), f32),
+                pltpu.VMEM((2, 2, rows // 4, cols, chans), bf16),
                 dma((frames,)), dma((6,)), dma((2, 3)),
                 dma((2, n_rw - 1)), dma((2, n_rw - 1)), dma((2, n_tm - 1)), dma((2, n_tm - 1)),
-                dma((2, 6, frames + 2)), dma((2, 6, frames + 2)),
+                dma((2, 6, frames + 2)), dma((2, 6, frames + 2)), dma((2, 3)), dma((2, 2)),
             ],
             compiler_params=pltpu.CompilerParams(
                 collective_id=0, has_side_effects=True, vmem_limit_bytes=52 << 20),

time: 54.6 us -> 53.3 us (0.976)
  the two profiles are of different devices: /device:TPU:3 before, /device:TPU:2 now
where the time goes in v5:
time: 53.3 us; the launch traced here: 53.2 us
  Pallas kernels  52.1 us (98%)
  local copies, waits for them, and re-layouts  1.15 us (2%)
    pallas_call x1, Pallas kernels, on_device(): pl.pallas_call(functools.partial(block_kernel, n_tm, n_rw, frames, rows,...  52.1 us
    unnamed x1, local copies, waits for them, and re-layouts  1.15 us

profile of v5, /device:TPU:2, one launch (start us, length us, event | category | flops | bytes accessed | tf_op | source)
XLA Modules:
  0.0 53.2 jit_solution(9112628649064174397)
XLA Ops:
  0.0 52.1 %shard_map.91 = bf16[4,16,48,256]{3,2,1,0:T(8,128)(2,1)S(1)} custom-call(bf16[4,16,48,256]{3,2,1,0:T(8,128)(2,1)} %feat.1, f32[1,256]{1,0:T(1,128)} %bitcast.10, f32[1,256]{1,0:T(1,128)} %bitcast.11, bf16[9,3,256,256]{3,2,1,0:T(8,128)(2,1)} %bitcast.8, f32[1,256]{1,0:T(1,128)} %bitcast.12, f32[1,256]{1,0:T(1,128)} %bitcast.13, f32[1,256]{1,0:T(1,128)} %bitcast.14, ...), custom_call_target="tpu_custom_call" | custom-call | tf_op jit(solution)/shard_map/pallas_call | solution.py:428
  52.1 1.1 %copy.11 = bf16[4,16,48,256]{3,2,1,0:T(8,128)(2,1)} copy(bf16[4,16,48,256]{3,2,1,0:T(8,128)(2,1)S(1)} %shard_map.91) | data formatting | bytes 3145728

commit v6 on v5

--- a/solution.py
+++ b/solution.py
@@ -27,7 +27,7 @@
 
 def block_kernel(n_tm, n_rw, frames, rows, cols, chans,
                  feat, g1, b1, w1, c1, g2, b2, w2, c2, out,
-                 fx, bx, xn, un, acc, wa, wb, va, vb, par, sl, ln, ra, tb, st, rel,
+                 fx, bx, xn, un, acc, wa, wb, va, vb, par, sl, ln, lt, ra, tb, st, rel,
                  lsem, psem, wsem, rsend, rrecv, tsend, trecv, hsend, hrecv, gsend, grecv):
     tm = lax.axis_index("tm")
     rw = lax.axis_index("rows")
@@ -47,8 +47,6 @@
     for c in taps:
         c.start()
 
-    tb[...] = jnp.zeros_like(tb)
-
     barrier = pltpu.get_barrier_semaphore()
     for k in range(1, n_rw):
         pl.semaphore_signal(barrier, 1, device_id=(tm, lax.rem(rw + k, n_rw)), device_id_type=MESH)
@@ -162,34 +160,42 @@
 
     def row_copy(n, k):
         return pltpu.make_async_remote_copy(
-            src_ref=ln.at[n], dst_ref=ra.at[n, k - 1], send_sem=rsend.at[n, k - 1], recv_sem=rrecv.at[n, k - 1],
+            src_ref=lt.at[n], dst_ref=ra.at[n, k - 1], send_sem=rsend.at[n], recv_sem=rrecv.at[n],
             device_id=(tm, lax.rem(rw + k, n_rw)), device_id_type=MESH)
 
     def time_copy(n, k):
         return pltpu.make_async_remote_copy(
-            src_ref=ln.at[2 + n], dst_ref=tb.at[n, k - 1], send_sem=tsend.at[n, k - 1], recv_sem=trecv.at[n, k - 1],
-            device_id=(tm + k, rw), device_id_type=MESH)
+            src_ref=ln.at[n], dst_ref=tb.at[n, k - 1], send_sem=tsend.at[n], recv_sem=trecv.at[n],
+            device_id=(lax.rem(tm + k, n_tm), rw), device_id_type=MESH)
+
+    def all_rows(n):
+        return pltpu.make_async_remote_copy(
+            src_ref=ra.at[n], dst_ref=ra.at[n], send_sem=rsend.at[n], recv_sem=rrecv.at[n],
+            device_id=(tm, lax.rem(rw + 1, n_rw)), device_id_type=MESH)
+
+    def all_times(n):
+        return pltpu.make_async_remote_copy(
+            src_ref=tb.at[n], dst_ref=tb.at[n], send_sem=tsend.at[n], recv_sem=trecv.at[n],
+            device_id=(lax.rem(tm + 1, n_tm), rw), device_id_type=MESH)
 
     def stats_start(n):
         ln[n] = pack(sl[n])
+        for k in (10, 6, 9, 11, 14, 2, 5, 7, 8, 12, 13, 15, 3, 4, 1):
+            time_copy(n, k).start()
+
+    def stats_finish(n, gain, shift, meanwhile):
+        all_times(n).wait_recv()
+        ago = lax.broadcasted_iota(jnp.int32, (n_tm - 1, 1, chans), 0) + 1
+        times = jnp.where(ago <= tm, tb[n], 0.0)
+        lt[n, 0] = jnp.sum(times[1:], axis=0)
+        lt[n, 1] = times[0]
+        lt[n, 2] = ln[n]
         for k in (4, 5, 3, 2, 6, 7, 1):
             row_copy(n, k).start()
-
-    def stats_finish(n, gain, shift, rest):
-        for k in range(1, n_rw):
-            row_copy(n, k).wait_recv()
-        line = ln[n] + jnp.sum(ra[n], axis=0)
-        ln[2 + n] = line
-        for k in (10, 6, 9, 11, 14, 2, 5, 7, 8, 12, 13, 15, 3, 4, 1):
-            @pl.when(tm + k < n_tm)
-            def _():
-                time_copy(n, k).start()
-        rest()
-        for k in range(1, n_tm):
-            @pl.when(tm >= k)
-            def _():
-                time_copy(n, k).wait_recv()
-        far, near, mine = unpack(jnp.sum(tb[n, 1:], axis=0)), unpack(tb[n, 0]), unpack(line)
+        meanwhile()
+        all_rows(n).wait_recv()
+        lines = lt[n] + jnp.sum(ra[n], axis=0)
+        far, near, mine = unpack(lines[0]), unpack(lines[1]), unpack(lines[2])
 
         def running(lo):
             total = jnp.sum(far[lo:lo + frames], axis=0, keepdims=True)
@@ -213,12 +219,8 @@
         st[2, 0:1] = 0.5 * shift
 
     def stats_sent(n):
-        for k in range(1, n_rw):
-            row_copy(n, k).wait_send()
-        for k in range(1, n_tm):
-            @pl.when(tm + k < n_tm)
-            def _():
-                time_copy(n, k).wait_send()
+        all_rows(n).wait_send()
+        all_times(n).wait_send()
 
     def normalise(buf, e):
         mean, scale, shift = st[0, pl.ds(e, 1), :], st[1, pl.ds(e, 1), :], st[2, 0:1]
@@ -308,11 +310,13 @@
         return y
 
     stats_start(0)
+    halo_start(fx, 0, EDGES, 1)
+    long_start(fx, 0, 0)
+    halo_start(fx, 0, EDGES, 0)
+    halo_start(fx, 0, MIDDLE, 1)
+    halo_start(fx, 0, MIDDLE[:1], 0)
     for e in range(2, 2 + frames):
         halo_start(fx, 0, ROW, e)
-    halo_start(fx, 0, EDGES, 1)
-    halo_start(fx, 0, EDGES[:1], 0)
-    long_start(fx, 0, 0)
     for c in small:
         c.wait()
     for c in taps[:3]:
@@ -320,24 +324,20 @@
     time_taps(wa, va)
 
     def rest_first():
-        halo_start(fx, 0, EDGES[1:], 0)
-        halo_start(fx, 0, MIDDLE, 1)
         for c in taps[3:]:
             c.wait()
         time_taps(wb, vb)
         long_start(fx, 0, 1)
 
-    def edges_on(buf, n):
-        for e in (1, 0):
-            halo_here(buf, n, EDGES, e)
-            halo_edge(buf, n, e)
+    def edges_on(buf, n, e):
+        halo_here(buf, n, EDGES, e)
+        halo_edge(buf, n, e)
 
     stats_finish(0, par[0], par[1], rest_first)
     for e in range(2, 2 + frames):
         halo_here(fx, 0, ROW, e)
         normalise(fx, e)
-    edges_on(fx, 0)
-    halo_start(fx, 0, MIDDLE[:1], 0)
+    edges_on(fx, 0, 1)
     long_start(fx, 0, 2)
 
     def earlier(buf, n, i, e):
@@ -363,6 +363,7 @@
         def _():
             halo_start(bx, 1, EDGES, 1)
             long_start(bx, 1, 0)
+            edges_on(fx, 0, 0)
 
         @pl.when(i == 1)
         def _():
@@ -374,16 +375,12 @@
 
     lax.fori_loop(0, 2, first_conv, 0)
 
-    def rest_second():
-        halo_start(bx, 1, EDGES[1:], 0)
-        halo_start(bx, 1, MIDDLE[:1], 1)
-        long_start(bx, 1, 2)
-
     stats_start(1)
-    halo_start(bx, 1, EDGES[:1], 0)
-    stats_finish(1, par[3], par[4], rest_second)
-    edges_on(bx, 1)
+    halo_start(bx, 1, EDGES, 0)
+    halo_start(bx, 1, MIDDLE[:1], 1)
     halo_start(bx, 1, MIDDLE, 0)
+    stats_finish(1, par[3], par[4], lambda: long_start(bx, 1, 2))
+    edges_on(bx, 1, 1)
     for e in range(2, 2 + frames):
         halo_here(bx, 1, ROW, e)
         normalise(bx, e)
@@ -397,6 +394,11 @@
 
         earlier(bx, 1, i, 1)
         put(f + 1, conv_late(wb, vb, f, par[5]))
+
+        @pl.when(i == 0)
+        def _():
+            edges_on(bx, 1, 0)
+
         earlier(bx, 1, i, 0)
         put(f, conv_early(wb, vb, f))
         return 0
@@ -442,13 +444,14 @@
                 pltpu.VMEM((3, chans, 3 * chans), bf16),
                 pltpu.VMEM((6, 1, chans), f32),
                 pltpu.VMEM((2, 2 * frames, chans), f32),
-                pltpu.VMEM((4, 1, chans), f32),
-                pltpu.VMEM((2, n_rw - 1, 1, chans), f32),
+                pltpu.VMEM((2, 1, chans), f32),
+                pltpu.VMEM((2, 3, 1, chans), f32),
+                pltpu.VMEM((2, n_rw - 1, 3, 1, chans), f32),
                 pltpu.VMEM((2, n_tm - 1, 1, chans), f32),
                 pltpu.VMEM((3, 8, chans), f32),
                 pltpu.VMEM((2, 2, rows // 4, cols, chans), bf16),
                 dma((frames,)), dma((6,)), dma((2, 3)),
-                dma((2, n_rw - 1)), dma((2, n_rw - 1)), dma((2, n_tm - 1)), dma((2, n_tm - 1)),
+                dma((2,)), dma((2,)), dma((2,)), dma((2,)),
                 dma((2, 6, frames + 2)), dma((2, 6, frames + 2)), dma((2, 3)), dma((2, 2)),
             ],
             compiler_params=pltpu.CompilerParams(

time: 53.3 us -> 52.1 us (0.977)
  the two profiles are of different devices: /device:TPU:2 before, /device:TPU:3 now
where the time goes in v6:
time: 52.1 us; the launch traced here: 51.2 us
  Pallas kernels  50 us (96%)
  local copies, waits for them, and re-layouts  1.15 us (2%)
    pallas_call x1, Pallas kernels, on_device(): pl.pallas_call(functools.partial(block_kernel, n_tm, n_rw, frames, rows,...  50 us
    unnamed x1, local copies, waits for them, and re-layouts  1.15 us

profile of v6, /device:TPU:3, one launch (start us, length us, event | category | flops | bytes accessed | tf_op | source)
XLA Modules:
  0.0 51.2 jit_solution(707928518291570992)
XLA Ops:
  0.0 50.0 %shard_map.91 = bf16[4,16,48,256]{3,2,1,0:T(8,128)(2,1)S(1)} custom-call(bf16[4,16,48,256]{3,2,1,0:T(8,128)(2,1)} %feat.1, f32[1,256]{1,0:T(1,128)} %bitcast.10, f32[1,256]{1,0:T(1,128)} %bitcast.11, bf16[9,3,256,256]{3,2,1,0:T(8,128)(2,1)} %bitcast.8, f32[1,256]{1,0:T(1,128)} %bitcast.12, f32[1,256]{1,0:T(1,128)} %bitcast.13, f32[1,256]{1,0:T(1,128)} %bitcast.14, ...), custom_call_target="tpu_custom_call" | custom-call | tf_op jit(solution)/shard_map/pallas_call | solution.py:430
  50.0 1.1 %copy.11 = bf16[4,16,48,256]{3,2,1,0:T(8,128)(2,1)} copy(bf16[4,16,48,256]{3,2,1,0:T(8,128)(2,1)S(1)} %shard_map.91) | data formatting | bytes 3145728

commit v7 on v6

--- a/solution.py
+++ b/solution.py
@@ -66,11 +66,11 @@
         loads[f].wait()
 
         def add_row(r, carry, f=f):
-            one, two = frame_sums(fx[2 + f, pl.ds(1 + 4 * r, 4)].reshape(4 * cols, chans).astype(jnp.float32))
+            one, two = frame_sums(fx[2 + f, pl.ds(1 + 8 * r, 8)].reshape(8 * cols, chans).astype(jnp.float32))
             return carry[0] + one, carry[1] + two
 
         zero = jnp.zeros((8, chans), jnp.float32)
-        one, two = lax.fori_loop(0, rows // 4, add_row, (zero, zero))
+        one, two = lax.fori_loop(0, rows // 8, add_row, (zero, zero))
         put_sums(0, f, one, two)
 
     pl.semaphore_wait(barrier, n_rw - 1 + n_tm - 1)
@@ -236,11 +236,11 @@
 
         @pl.when(there)
         def _():
-            def four(i, _):
-                for r in range(1, 5):
-                    one(r + 4 * i)
+            def eight(i, _):
+                for r in range(1, 9):
+                    one(r + 8 * i)
                 return 0
-            lax.fori_loop(0, rows // 4, four, 0)
+            lax.fori_loop(0, rows // 8, eight, 0)
 
         @pl.when(there & (rw > 0))
         def _():
@@ -272,13 +272,14 @@
     def frame(e):
         return xn[e].astype(jnp.float32)
 
-    col = lax.broadcasted_iota(jnp.int32, (pix, chans), 0) % cols
-
-    def product(w, v, k, e):
+    half_pix = pix // 2
+    col = lax.broadcasted_iota(jnp.int32, (half_pix, chans), 0) % cols
+
+    def product(w, v, k, e, at):
         total = None
         for a in range(3):
             tap = (w.at[a * 3], w.at[a * 3 + 1], v.at[a], w.at[a * 3 + 2])[k]
-            part = jnp.dot(un[k, a * cols:a * cols + pix, :], tap[:, e * chans:(e + 1) * chans],
+            part = jnp.dot(un[k, at + a * cols:at + a * cols + half_pix, :], tap[:, e * chans:(e + 1) * chans],
                            preferred_element_type=jnp.float32)
             total = part if total is None else total + part
         return total
@@ -287,7 +288,7 @@
         if e == 0:
             return jnp.where(col == 0, 0.0, pltpu.roll(y, 1, 0))
         if e == 2:
-            return jnp.where(col == cols - 1, 0.0, pltpu.roll(y, pix - 1, 0))
+            return jnp.where(col == cols - 1, 0.0, pltpu.roll(y, half_pix - 1, 0))
         return y
 
     def conv_late(w, v, f, bias):
@@ -295,19 +296,25 @@
         un[1] = (d1 + d2).astype(jnp.bfloat16)
         un[2] = (d2 - d1).astype(jnp.bfloat16)
         un[3] = (d1 - d3).astype(jnp.bfloat16)
-        y0 = y1 = bias
-        for e in (1, 0, 2):
-            m1, m2, m3 = [product(w, v, k, e) for k in (1, 2, 3)]
-            y0, y1 = y0 + column(m1 + m2, e), y1 + column(m1 - m2 - m3, e)
-        acc[...] = y0
-        return y1
+        parts = []
+        for at in (0, half_pix):
+            y0 = y1 = bias
+            for e in (1, 0, 2):
+                m1, m2, m3 = [product(w, v, k, e, at) for k in (1, 2, 3)]
+                y0, y1 = y0 + column(m1 + m2, e), y1 + column(m1 - m2 - m3, e)
+            acc[at:at + half_pix] = y0
+            parts.append(y1)
+        return jnp.concatenate(parts, axis=0)
 
     def conv_early(w, v, f):
         un[0] = (frame(f) - frame(f + 2)).astype(jnp.bfloat16)
-        y = acc[...]
-        for e in (1, 0, 2):
-            y = y + column(product(w, v, 0, e), e)
-        return y
+        parts = []
+        for at in (0, half_pix):
+            y = acc[at:at + half_pix]
+            for e in (1, 0, 2):
+                y = y + column(product(w, v, 0, e, at), e)
+            parts.append(y)
+        return jnp.concatenate(parts, axis=0)
 
     stats_start(0)
     halo_start(fx, 0, EDGES, 1)
@@ -361,7 +368,6 @@
 
         @pl.when(i == 0)
         def _():
-            halo_start(bx, 1, EDGES, 1)
             long_start(bx, 1, 0)
             edges_on(fx, 0, 0)
 
@@ -376,6 +382,7 @@
     lax.fori_loop(0, 2, first_conv, 0)
 
     stats_start(1)
+    halo_start(bx, 1, EDGES, 1)
     halo_start(bx, 1, EDGES, 0)
     halo_start(bx, 1, MIDDLE[:1], 1)
     halo_start(bx, 1, MIDDLE, 0)

time: 52.1 us -> 50.5 us (0.969)
  Pallas kernels: 50 us -> 48.4 us
    pallas_call x1, Pallas kernels: 50 us -> 48.4 us  [on_device(): pl.pallas_call(functools.partial(block_kernel, n_tm, n_rw, frames, rows,...]
where the time goes in v7:
time: 50.5 us; the launch traced here: 49.5 us
  Pallas kernels  48.4 us (96%)
  local copies, waits for them, and re-layouts  1.15 us (2%)
    pallas_call x1, Pallas kernels, on_device(): pl.pallas_call(functools.partial(block_kernel, n_tm, n_rw, frames, rows,...  48.4 us
    unnamed x1, local copies, waits for them, and re-layouts  1.15 us

profile of v7, /device:TPU:3, one launch (start us, length us, event | category | flops | bytes accessed | tf_op | source)
XLA Modules:
  0.0 49.5 jit_solution(16232354332423017072)
XLA Ops:
  0.0 48.4 %shard_map.91 = bf16[4,16,48,256]{3,2,1,0:T(8,128)(2,1)S(1)} custom-call(bf16[4,16,48,256]{3,2,1,0:T(8,128)(2,1)} %feat.1, f32[1,256]{1,0:T(1,128)} %bitcast.10, f32[1,256]{1,0:T(1,128)} %bitcast.11, bf16[9,3,256,256]{3,2,1,0:T(8,128)(2,1)} %bitcast.8, f32[1,256]{1,0:T(1,128)} %bitcast.12, f32[1,256]{1,0:T(1,128)} %bitcast.13, f32[1,256]{1,0:T(1,128)} %bitcast.14, ...), custom_call_target="tpu_custom_call" | custom-call | tf_op jit(solution)/shard_map/pallas_call | solution.py:437
  48.4 1.1 %copy.11 = bf16[4,16,48,256]{3,2,1,0:T(8,128)(2,1)} copy(bf16[4,16,48,256]{3,2,1,0:T(8,128)(2,1)S(1)} %shard_map.91) | data formatting | bytes 3145728

commit v8 on v7

--- a/solution.py
+++ b/solution.py
@@ -272,14 +272,14 @@
     def frame(e):
         return xn[e].astype(jnp.float32)
 
-    half_pix = pix // 2
-    col = lax.broadcasted_iota(jnp.int32, (half_pix, chans), 0) % cols
+    chunk = pix // 4
+    col = lax.broadcasted_iota(jnp.int32, (chunk, chans), 0) % cols
 
     def product(w, v, k, e, at):
         total = None
         for a in range(3):
             tap = (w.at[a * 3], w.at[a * 3 + 1], v.at[a], w.at[a * 3 + 2])[k]
-            part = jnp.dot(un[k, at + a * cols:at + a * cols + half_pix, :], tap[:, e * chans:(e + 1) * chans],
+            part = jnp.dot(un[k, at + a * cols:at + a * cols + chunk, :], tap[:, e * chans:(e + 1) * chans],
                            preferred_element_type=jnp.float32)
             total = part if total is None else total + part
         return total
@@ -288,7 +288,7 @@
         if e == 0:
             return jnp.where(col == 0, 0.0, pltpu.roll(y, 1, 0))
         if e == 2:
-            return jnp.where(col == cols - 1, 0.0, pltpu.roll(y, half_pix - 1, 0))
+            return jnp.where(col == cols - 1, 0.0, pltpu.roll(y, chunk - 1, 0))
         return y
 
     def conv_late(w, v, f, bias):
@@ -297,20 +297,20 @@
         un[2] = (d2 - d1).astype(jnp.bfloat16)
         un[3] = (d1 - d3).astype(jnp.bfloat16)
         parts = []
-        for at in (0, half_pix):
+        for at in range(0, pix, chunk):
             y0 = y1 = bias
             for e in (1, 0, 2):
                 m1, m2, m3 = [product(w, v, k, e, at) for k in (1, 2, 3)]
                 y0, y1 = y0 + column(m1 + m2, e), y1 + column(m1 - m2 - m3, e)
-            acc[at:at + half_pix] = y0
+            acc[at:at + chunk] = y0
             parts.append(y1)
         return jnp.concatenate(parts, axis=0)
 
     def conv_early(w, v, f):
         un[0] = (frame(f) - frame(f + 2)).astype(jnp.bfloat16)
         parts = []
-        for at in (0, half_pix):
-            y = acc[at:at + half_pix]
+        for at in range(0, pix, chunk):
+            y = acc[at:at + chunk]
             for e in (1, 0, 2):
                 y = y + column(product(w, v, 0, e, at), e)
             parts.append(y)

time: 50.5 us -> 50.5 us (level)
  no operation moved by 1% of the time
where the time goes in v8:
time: 50.5 us; the launch traced here: 49.6 us
  Pallas kernels  48.4 us (96%)
  local copies, waits for them, and re-layouts  1.15 us (2%)
    pallas_call x1, Pallas kernels, on_device(): pl.pallas_call(functools.partial(block_kernel, n_tm, n_rw, frames, rows,...  48.4 us
    unnamed x1, local copies, waits for them, and re-layouts  1.15 us

profile of v8, /device:TPU:3, one launch (start us, length us, event | category | flops | bytes accessed | tf_op | source)
XLA Modules:
  0.0 49.6 jit_solution(13571182966925314055)
XLA Ops:
  0.0 48.4 %shard_map.91 = bf16[4,16,48,256]{3,2,1,0:T(8,128)(2,1)S(1)} custom-call(bf16[4,16,48,256]{3,2,1,0:T(8,128)(2,1)} %feat.1, f32[1,256]{1,0:T(1,128)} %bitcast.10, f32[1,256]{1,0:T(1,128)} %bitcast.11, bf16[9,3,256,256]{3,2,1,0:T(8,128)(2,1)} %bitcast.8, f32[1,256]{1,0:T(1,128)} %bitcast.12, f32[1,256]{1,0:T(1,128)} %bitcast.13, f32[1,256]{1,0:T(1,128)} %bitcast.14, ...), custom_call_target="tpu_custom_call" | custom-call | tf_op jit(solution)/shard_map/pallas_call | solution.py:437
  48.4 1.1 %copy.11 = bf16[4,16,48,256]{3,2,1,0:T(8,128)(2,1)} copy(bf16[4,16,48,256]{3,2,1,0:T(8,128)(2,1)S(1)} %shard_map.91) | data formatting | bytes 3145728
